TPU v7x, 32 devices: a whole 2x2x4 slice. The times are simulated.
32 devices in a mesh: grp: 2 (over x), slc: 16 (over z, y, core).
Axes of the slice: x: 2, y: 2, z: 4, core: 2. Of those that a mesh axis runs over, the one named last changes fastest.
Arguments:
- kspace: bfloat16 [4, 32, 16, 16384], P('grp', None, None, 'slc'), parts along dimension 0, may hold values from -6 to 6
- coil_maps: bfloat16 [4, 32, 16, 128, 128], P('grp', 'slc'), parts along dimension 0, may hold values from -1 to 1, as said below
- sample_mask: int32 [64, 16, 128], P('grp'), parts along dimension 0, may hold values 0 or 1
- tap_order: int32 [27], replicated, may hold values from 0 to 26, each once
- first_kernel: bfloat16 [27, 2, 64], replicated, may hold values from -0.875 to 0.875
- first_bias: float32 [64], replicated, may hold values from -2 to 2
- second_kernel: bfloat16 [27, 64, 2], replicated, may hold values from -0.15625 to 0.15625
- second_bias: float32 [2], replicated, may hold values from -2 to 2
Outputs:
- estimate: float32 [4, 32, 128, 128], P('grp', 'slc'), parts along dimension 0
- dual_var: float32 [4, 32, 128, 128], P('grp', 'slc'), parts along dimension 0
There are 2 independent parts, one for each index of `grp`. A program takes and returns all parts, laid end to end along the dimension named above; an argument that names none is the same for every part. Nothing has to cross between parts.
Inputs may be any that keep to these rules, and one draw needn't show every extreme that they name: `coil_maps`: at every cell the squared real and imaginary parts of the maps summed over the 16 coils make one, up to rounding. `tap_order`: each tap index appears exactly once.
All inputs are finite; a program needn't handle non-finite values.
Results may differ from a plain program's by a relative error of at most 0.014.
Values may be sent and summed in bfloat16 or wider, within the bound.
No kernel may reach another device: no remote copies, remote signals or barrier semaphores. Data moves between devices by JAX's collectives and lax.ppermute only.
A program may use at most 128 MiB of HBM per device.

v0:
```python
import functools
import math

import jax
import jax.numpy as jnp
import numpy as np
from jax import lax
from jax.experimental import pallas as pl
from jax.experimental.pallas import tpu as pltpu
from jax.sharding import PartitionSpec as P

GROUP = 8
STEP = 4
SETS = 2
AT_ONCE = 16
MAPS_AT_ONCE = 4
LOW = jnp.bfloat16
FULL = jnp.float32
VMEM = pl.BlockSpec(memory_space=pltpu.VMEM)
SMEM = pl.BlockSpec(memory_space=pltpu.SMEM)


def make_table(length, direction):
    positions = np.arange(length)
    angles = 2.0 * math.pi / length * (positions[:, None] * positions[None, :] % length)
    real_t = np.cos(angles) / math.sqrt(length)
    imag_t = direction * np.sin(angles) / math.sqrt(length)
    upper = np.stack([real_t, imag_t], axis=1)
    lower = np.stack([-imag_t, real_t], axis=1)
    return np.stack([upper, lower]).astype(np.float32)


def spread_table(table, copies):
    size = 2 * table.shape[1]
    return np.kron(table.reshape(size, size).T, np.eye(copies, dtype=np.float32))


def low(table):
    return jnp.asarray(table, LOW)


def tap_kernel(tap_order, stored):
    chosen = (tap_order[None, :] == jnp.arange(27, dtype=jnp.int32)[:, None]).astype(LOW)
    return einsum("tq,qio->tio", chosen, stored).astype(LOW)


def einsum(pattern, a, b):
    return jnp.einsum(pattern, a, b, preferred_element_type=FULL)


def swap(blocks):
    return lax.all_to_all(blocks, "slc", split_axis=0, concat_axis=0, tiled=True)


def matmul(a, b, dims=((1,), (0,))):
    return lax.dot_general(a, b, (dims, ((), ())), preferred_element_type=FULL)


def maps_kernel(place_ref, m_ref, *refs):
    _, depth, coils, H, W = m_ref.shape
    outs, scratch = refs[:-1], refs[-1]
    n = len(outs)
    part = W // (n * SETS)
    for c in range(coils):
        for p in range(2):
            turned = [
                jnp.transpose(m_ref[p, z, c]).astype(FULL).reshape(n, SETS * part, H) for z in range(depth)
            ]
            for i in range(SETS):
                rows = [t[:, i * part : (i + 1) * part] for t in turned]
                scratch[:, i, c, p] = jnp.concatenate(rows, axis=1).astype(LOW)
    for k in range(n):
        outs[k][...] = scratch[lax.rem(place_ref[0] + k, n)]


def maps_step(place, coil_maps, n):
    _, depth, coils, H, W = coil_maps.shape
    rows = depth * W // (n * SETS)
    return pl.pallas_call(
        maps_kernel,
        grid=(coils // MAPS_AT_ONCE,),
        out_shape=[jax.ShapeDtypeStruct((SETS, coils, 2, rows, H), LOW)] * n,
        in_specs=[SMEM, pl.BlockSpec((2, depth, MAPS_AT_ONCE, H, W), lambda i: (0, 0, i, 0, 0))],
        out_specs=[pl.BlockSpec((SETS, MAPS_AT_ONCE, 2, rows, H), lambda i: (0, i, 0, 0, 0))] * n,
        scratch_shapes=[pltpu.VMEM((n, SETS, MAPS_AT_ONCE, 2, rows, H), LOW)],
    )(place, coil_maps)


def point_kernel(place_ref, k_ref, mask_ref, table_ref, depth_ref, *refs):
    _, slices, coils, _ = k_ref.shape
    whole, by_x, turned = refs[0], refs[-2], refs[-1]
    n, _, twice, _ = whole.shape
    lines = twice // 2
    W = table_ref.shape[0] // 2
    cols = W // n

    @pl.loop(0, slices)
    def _(z):
        rows = jnp.concatenate(
            [
                jnp.concatenate([k_ref[p, z, :, r * W : (r + 1) * W] for p in range(2)], axis=1)
                for r in range(lines)
            ],
            axis=0,
        )
        image = matmul(table_ref[...], rows, ((1,), (1,))) * mask_ref[pl.ds(z, 1), :]
        for p in range(2):
            by_x[:, p, z] = image[p * W : (p + 1) * W].reshape(n, cols, lines * coils)

    tiles, lane = turned.shape[1], turned.shape[3]
    each = tiles // SETS
    for k in range(n):
        d = lax.rem(place_ref[0] + k, n)
        own = by_x[d].reshape(2 * slices * cols, lines * coils).astype(LOW)
        full = matmul(own, depth_ref[...], ((0,), (0,)))
        for t in range(tiles):
            turned[k % 2, t] = full[:, t * lane : (t + 1) * lane]
        for c in range(coils):
            picked = [turned[k % 2, t, pl.ds(c, lines, stride=coils), :] for t in range(tiles)]
            for i in range(SETS):
                both = [
                    jnp.concatenate(picked[i * each + q * each // 2 :][: each // 2], axis=1)
                    for q in range(2)
                ]
                block = jnp.concatenate(both, axis=0).astype(LOW)
                if i == 0:
                    whole[d, c] = block
                else:
                    refs[1 + (i - 1) * n + k][c] = block


def point_step(place, kspace, mask, table, depth_table, n):
    _, slices, coils, points = kspace.shape
    W = table.shape[0] // 2
    lines, cols = points // W, W // n
    block = (coils, 2 * lines, slices * cols // SETS)
    return pl.pallas_call(
        point_kernel,
        out_shape=[jax.ShapeDtypeStruct((n, *block), LOW)] + [jax.ShapeDtypeStruct(block, LOW)] * (n * (SETS - 1)),
        in_specs=[SMEM] + [VMEM] * 4,
        out_specs=[VMEM] * (1 + n * (SETS - 1)),
        scratch_shapes=[
            pltpu.VMEM((n, 2, slices, cols, lines * coils), FULL),
            pltpu.VMEM((2, 2 * slices * cols // W, lines * coils, W), FULL),
        ],
    )(place, kspace, mask, table, depth_table)


def data_kernel(turn, n, place_ref, mask_ref, back_src, fwd, back, zf_ref, zb_ref, *refs):
    (out_ref, s_ref, ad_ref, sum_ref), sent = refs[-4:], refs[:-4]
    if len(sent) > n + 1:
        sent, u_ref = sent[:-1], sent[-1]
    _, coils, _, depth_cols, H = s_ref.shape
    rows = n * depth_cols
    for k in range(n):
        source = lax.rem(place_ref[0] + n - k, n)
        s_ref[source] = sent[k][turn]
        if len(sent) == 2 * n:
            u_ref[source] = sent[n + k][...]
    if len(sent) == n + 1:
        u_ref = sent[n]
    lines = u_ref.shape[2] // 2

    def sens(c):
        return [s_ref[:, c, p].astype(FULL).reshape(rows, H) for p in range(2)]

    def combine(total_ref, first, image):
        real, imag = total_ref[0], total_ref[1]
        for k in range(AT_ONCE):
            s = sens(first + k)
            r, i = image[k * rows : (k + 1) * rows, :H], image[k * rows : (k + 1) * rows, H:]
            real += s[0] * r + s[1] * i
            imag += s[0] * i - s[1] * r
        total_ref[0], total_ref[1] = real, imag

    ad_ref[...] = jnp.zeros_like(ad_ref)
    sum_ref[...] = jnp.zeros_like(sum_ref)

    @pl.loop(0, coils // AT_ONCE)
    def _(g):
        first = g * AT_ONCE
        u = [u_ref[:, first + k].reshape(n * 2 * lines, rows) for k in range(AT_ONCE)]
        combine(ad_ref, first, matmul(jnp.concatenate(u, axis=1), back_src[...], ((0,), (0,))))

    @pl.loop(0, coils // AT_ONCE)
    def _(g):
        first = g * AT_ONCE
        v = [ad_ref[0], ad_ref[1]]
        many = []
        for k in range(AT_ONCE):
            s = sens(first + k)
            both = [s[0] * v[0] - s[1] * v[1], s[0] * v[1] + s[1] * v[0]]
            many.append(jnp.concatenate(both, axis=1).astype(LOW))
        f = matmul(jnp.concatenate(many, axis=0), fwd[...]).astype(LOW)
        wide = []
        for k in range(AT_ONCE):
            part = f[k * rows : (k + 1) * rows]
            wide.append(jnp.concatenate([part[:, :H], part[:, H:]], axis=0))
        freq = matmul(zf_ref[...], jnp.concatenate(wide, axis=1))
        keep = []
        for k in range(AT_ONCE):
            part = freq[:, k * H : (k + 1) * H]
            m = mask_ref[first + k]
            keep.append(jnp.concatenate([part[:rows] * m, part[rows:] * m], axis=0))
        h = matmul(zb_ref[...], jnp.concatenate(keep, axis=1).astype(LOW)).astype(LOW)
        many = []
        for k in range(AT_ONCE):
            part = h[:, k * H : (k + 1) * H]
            many.append(jnp.concatenate([part[:rows], part[rows:]], axis=1))
        combine(sum_ref, first, matmul(jnp.concatenate(many, axis=0), back[...]))

    tall = out_ref.shape[2]
    edge = (tall - depth_cols) // 2
    for q in range(2):
        blank = jnp.zeros((edge, H), FULL)
        update = jnp.concatenate([blank, 2.0 * ad_ref[q] - sum_ref[q], blank], axis=0)
        for d in range(n):
            out_ref[d, q] = update[d * depth_cols : d * depth_cols + tall].astype(LOW)


def data_step(turn, n, place, maps, spectra, mask, tables):
    _, coils, _, depth_cols, H = maps[0].shape
    rows = n * depth_cols
    halo = 4 * (GROUP // SETS)
    scratch = [
        pltpu.VMEM((n, coils, 2, depth_cols, H), LOW),
        pltpu.VMEM((2, rows, H), FULL),
        pltpu.VMEM((2, rows, H), FULL),
    ]
    if len(spectra) == n:
        kernel = functools.partial(data_kernel_blocks, turn, n)
        scratch = scratch + [pltpu.VMEM((n, *spectra[0].shape), LOW)]
    else:
        kernel = functools.partial(data_kernel, turn, n)
    return pl.pallas_call(
        kernel,
        out_shape=jax.ShapeDtypeStruct((n, 2, depth_cols + halo, H), LOW),
        in_specs=[SMEM] + [VMEM] * (1 + len(tables) + n + len(spectra)),
        out_specs=VMEM,
        scratch_shapes=scratch,
    )(place, mask, *tables, *maps, *spectra)


def data_kernel_blocks(turn, n, *refs):
    data_kernel(turn, n, *refs[:-5], refs[-1], *refs[-5:-1])


def data_step_plain(maps, spectra, mask, table_f, table_g, depth_f, depth_g):
    n, coils, _, depth, cols, H = maps.shape
    slices = n * depth
    sens = maps.astype(FULL).transpose(2, 1, 4, 0, 3, 5).reshape(2, coils, cols, slices, H)
    part = spectra.reshape(n, coils, 2, H // n, slices, cols)
    part = part.transpose(2, 1, 5, 4, 0, 3).reshape(2, coils, cols, slices, H)

    def combine(image):
        return jnp.stack([
            jnp.sum(sens[0] * image[0] + sens[1] * image[1], axis=0),
            jnp.sum(sens[0] * image[1] - sens[1] * image[0], axis=0),
        ])

    v = combine(einsum("pcxzj,pjqk->qcxzk", part, table_g))
    w = jnp.stack([sens[0] * v[0] - sens[1] * v[1], sens[0] * v[1] + sens[1] * v[0]]).astype(LOW)
    f = einsum("pcxzj,pjqk->qcxzk", w, table_f).astype(LOW)
    g = einsum("pcxjk,pjqz->qcxzk", f, depth_f) * mask[:, None]
    h = einsum("pcxjk,pjqz->qcxzk", g.astype(LOW), depth_g).astype(LOW)
    update = 2.0 * v - combine(einsum("pcxzj,pjqk->qcxzk", h, table_g))
    padded = jnp.pad(update.astype(LOW), ((0, 0), (0, 0), (2, 2), (0, 0)))
    sent = jnp.stack([padded[:, :, d * depth : d * depth + depth + 4] for d in range(n)])
    return sent.transpose(0, 1, 3, 2, 4)


def denoise_kernel(base_ref, wa_ref, wb_ref, one_ref, two_ref, last_ref, est_ref, dual_ref, cols, acc):
    blocks, _, tall, L = wa_ref.shape
    part = GROUP // SETS
    window = tall // part
    R = blocks * GROUP
    depth = window - 4
    slices = base_ref[1]
    lane = lax.broadcasted_iota(jnp.int32, (R, L), 1)
    row = lax.broadcasted_iota(jnp.int32, (R, L), 0)

    def field(i, z):
        both = [
            ref[:, i].astype(FULL)[:, z * part : (z + 1) * part] for ref in (wa_ref, wb_ref)
        ]
        return jnp.concatenate(both, axis=1).reshape(R, L)

    for z in range(window):
        moved = ([], [])
        for i in range(2):
            f = field(i, z)
            moved[0].append(jnp.where(row < 2, 0.0, pltpu.roll(f, 2, axis=0)))
            moved[1].append(jnp.where(row >= R - 2, 0.0, pltpu.roll(f, R - 2, axis=0)))
        for phase in range(2):
            for side in range(3):
                parts = []
                for f in moved[phase]:
                    if side == 0:
                        f = jnp.where(lane == 0, 0.0, pltpu.roll(f, 1, axis=1))
                    if side == 2:
                        f = jnp.where(lane == L - 1, 0.0, pltpu.roll(f, L - 1, axis=1))
                    parts.append(f.reshape(blocks, GROUP, L))
                cols[phase, z, side] = jnp.concatenate(parts, axis=1).astype(LOW)

    small_lane = lax.broadcasted_iota(jnp.int32, (2 * GROUP, L), 1)
    ones = jnp.where(lax.broadcasted_iota(jnp.int32, (2 * GROUP, 2 * L), 0) < 3, 1.0, 0.0).astype(LOW)

    def live(k):
        z = base_ref[0] - 1 + k
        return jnp.where((z >= 0) & (z < slices), 1.0, 0.0).astype(FULL)

    first_live, last_live = live(0), live(window - 3)

    @pl.loop(0, blocks)
    def _(j):
        for phase in range(2):

            def gathered(k):
                return jnp.concatenate(
                    [cols[phase, k + a, b, j] for a in range(3) for b in range(3)], axis=0
                )

            hidden = []
            for k in range(2):
                patch = jnp.concatenate([gathered(2 * k), gathered(2 * k + 1)], axis=1)
                summed = matmul(one_ref[...], jnp.concatenate([patch, ones], axis=0))
                hidden.append(jnp.maximum(summed, 0.0))
            edge = [(hidden[0][:, :L] * first_live).astype(LOW), (hidden[1][:, L:] * last_live).astype(LOW)]
            inner = [hidden[0][:, L:].astype(LOW), hidden[1][:, :L].astype(LOW)]
            hidden = [
                jnp.concatenate([edge[0], inner[0]], axis=1),
                jnp.concatenate([inner[1], edge[1]], axis=1),
            ]
            width = 2 * GROUP
            middle = jnp.concatenate([inner[0], inner[1]], axis=1)
            terms = matmul(two_ref[...], jnp.concatenate([hidden[0], middle, hidden[1]], axis=0))
            for z in range(2):
                left, mid, right = [
                    terms[i * width : (i + 1) * width, z * L : (z + 1) * L] for i in range(3)
                ]
                left = jnp.where(small_lane == 0, 0.0, pltpu.roll(left, 1, axis=1))
                right = jnp.where(small_lane == L - 1, 0.0, pltpu.roll(right, L - 1, axis=1))
                both = left + mid + right
                for o in range(2):
                    acc[phase, z, o, j] = both[o * GROUP : (o + 1) * GROUP]

    for z in range(depth):
        for o in range(2):
            even = pltpu.roll(acc[0, z, o].reshape(R, L), R - 2, axis=0)
            odd = pltpu.roll(acc[1, z, o].reshape(R, L), 2, axis=0)
            noise = jnp.where(row >= R - 2, 0.0, even) + jnp.where(row < 2, 0.0, odd) + last_ref[o]
            est_ref[o, z] = jnp.transpose(field(o, z + 2) - noise)
            dual_ref[o, z] = jnp.transpose(noise)


def denoise(base, windows, one, bias, two, last):
    blocks, _, tall, L = windows[0].shape
    spread = tall * SETS // GROUP
    depth = spread - 4
    R = blocks * GROUP
    taps_one = one.reshape(3, 3, 3, 2, -1)
    taps_two = two.reshape(3, 3, 3, -1, 2)
    hid = taps_one.shape[-1]
    dx, rr, rb = jnp.arange(3), jnp.arange(GROUP), jnp.arange(STEP)
    into = (dx[:, None, None] == rr[None, :, None] - rb[None, None, :] - 1).astype(LOW)
    out = (dx[:, None, None] == rb[None, None, :] - rr[None, :, None] + 3).astype(LOW)
    first = einsum("abxio,xrk->koabir", taps_one, into).astype(LOW).reshape(STEP * hid, 18 * GROUP)
    second = einsum("abxoc,xrk->bcrako", taps_two, out).astype(LOW).reshape(6 * GROUP, 3 * STEP * hid)
    terms, left = [], jnp.tile(bias, STEP)
    for _ in range(3):
        terms.append(lax.reduce_precision(left, 8, 7))
        left = left - terms[-1]
    terms = jnp.stack(terms, axis=1).astype(LOW)
    first = jnp.concatenate([first, jnp.pad(terms, ((0, 0), (0, 2 * GROUP - 3)))], axis=1)
    shape = jax.ShapeDtypeStruct((2, depth, L, R), FULL)
    return pl.pallas_call(
        denoise_kernel,
        out_shape=(shape, shape),
        in_specs=[SMEM, VMEM, VMEM, VMEM, VMEM, SMEM],
        out_specs=(VMEM, VMEM),
        scratch_shapes=[
            pltpu.VMEM((2, spread, 3, blocks, 2 * GROUP, L), LOW),
            pltpu.VMEM((2, depth, 2, blocks, GROUP, L), FULL),
        ],
    )(base, *windows, first, second, last)


def on_device(
    kspace, coil_maps, sample_mask, tap_order, first_kernel, first_bias, second_kernel, second_bias
):
    n = lax.axis_size("slc")
    position = lax.axis_index("slc")
    _, depth, coils, H, W = coil_maps.shape
    slices, points = kspace.shape[1], kspace.shape[3]
    lines = points // W
    ncol = W // n

    fits = ncol == GROUP and coils * lines == W and coils % AT_ONCE == 0
    table_f, table_g = make_table(H, -1.0), make_table(H, 1.0)
    depth_f, depth_g = make_table(slices, -1.0), make_table(slices, 1.0)
    mask = sample_mask.astype(FULL).transpose(1, 0, 2)
    own_mask = lax.dynamic_slice_in_dim(sample_mask, position * lines, lines, axis=2)
    if fits:
        part = ncol // SETS
        place = position.astype(jnp.int32)[None]

        def send(blocks):
            got = list(blocks)
            for k in sorted(range(1, n), key=lambda k: abs(2 * k - n)):
                got[k] = lax.ppermute(blocks[k], "slc", [(i, (i + k) % n) for i in range(n)])
            return got

        maps = maps_step(place, coil_maps, n)
        maps = send(maps)
        own_mask = own_mask.transpose(0, 2, 1).reshape(slices, lines * coils).astype(FULL)
        table_x = make_table(W, 1.0).reshape(2 * W, 2 * W)
        depth_t = spread_table(depth_g, ncol).T
        depth_t = depth_t.reshape(-1, 2, slices, SETS, part).transpose(0, 3, 1, 2, 4).reshape(depth_t.shape)
        by_z = point_step(place, kspace, own_mask, low(table_x.T), low(depth_t), n)
        back_src = table_g.reshape(2, n, lines, 2 * H).transpose(1, 0, 2, 3).reshape(2 * H, 2 * H)
        tables = [
            low(table)
            for table in (
                back_src,
                table_f.reshape(2 * H, 2 * H),
                table_g.reshape(2 * H, 2 * H),
                spread_table(depth_f, part),
                spread_table(depth_g, part),
            )
        ]
        tall_mask = jnp.repeat(mask, part, axis=1)
        first = by_z[0]
        first = [swap(first)]
        later, tall_mask, maps = lax.optimization_barrier((by_z[1:], tall_mask, maps))
        later = send(later)
        windows = []
        for i, spectra in enumerate((first, later)):
            sent = data_step(i, n, place, maps, spectra, tall_mask, tables)
            if i == 0:
                _, later[:] = lax.optimization_barrier((sent, later))
            windows.append(swap(sent))
    else:
        maps = coil_maps.reshape(2, depth, coils, H, n, ncol).transpose(4, 2, 0, 1, 5, 3)
        maps = swap(maps)
        masked = kspace.reshape(2, slices, coils, lines, W) * own_mask.astype(LOW)[None, ..., None]
        by_x = einsum("pzcrj,pjqk->qzcrk", masked, low(make_table(W, 1.0))).astype(LOW)
        by_z = einsum("pjcrx,pjqk->xcqrk", by_x, low(depth_g)).astype(LOW)
        by_z = by_z.reshape(n, ncol, coils, 2 * lines, slices).transpose(0, 2, 3, 4, 1)
        spectra = swap(by_z.reshape(n, coils, 2 * lines, slices * ncol))
        got = swap(data_step_plain(maps, spectra, mask, *map(low, (table_f, table_g, depth_f, depth_g))))
        got = got.transpose(0, 3, 1, 2, 4).reshape(W // GROUP, SETS, GROUP // SETS, 2, depth + 4, H)
        got = got.transpose(1, 0, 3, 4, 2, 5).reshape(SETS, W // GROUP, 2, -1, H)
        windows = [got[i] for i in range(SETS)]

    kernel_one = tap_kernel(tap_order, first_kernel)
    kernel_two = tap_kernel(tap_order, second_kernel)
    base = jnp.stack([position * depth, jnp.int32(slices)]).astype(jnp.int32)
    return denoise(base, windows, kernel_one, first_bias, kernel_two, second_bias)


def solution(mesh):
    placed = (
        P("grp", None, None, "slc"),
        P("grp", "slc", None, None, None),
        P("grp", None, None),
        P(),
        P(),
        P(),
        P(),
        P(),
    )
    return jax.shard_map(
        on_device,
        mesh=mesh,
        in_specs=placed,
        out_specs=(P("grp", "slc", None, None), P("grp", "slc", None, None)),
        check_vma=False,
    )
```

profile of v0, /device:TPU:0, one launch (start us, length us, event | category | flops | bytes accessed | tf_op | source)
XLA Modules:
  0.0 174.2 jit_solution(17724127054846896024)
XLA Ops:
  0.6 1.1 convert_bitcast_fusion.1
  1.9 0.7 copy.40.mask_ref
  2.6 11.3 %shard_map.158 = (bf16[16,16,16,128]{3,2,1,0:T(8,128)(2,1)}, bf16[16,16,128]{2,1,0:T(8,128)(2,1)}, bf16[16,16,128]{2,1,0:T(8,128)(2,1)}, bf16[16,16,128]{2,1,0:T...) custom-call(s32[1]{0:T(128)} %bitcast.1.place_ref.refs_0_, ...), custom_call_target="tpu_custom_call" | custom-call | tf_op jit(solution)/shard_map/pallas_call | solution.py:137
  13.9 7.6 %all-to-all-start = ((bf16[16,16,16,128]{3,2,1,0:T(8,128)(2,1)}), bf16[16,16,16,128]{3,2,1,0:T(8,128)(2,1)S(1)}, u32[]{:S(2)}, u32[]{:S(2)}) async-start(bf16[16,16,16,128]{3,2,1,0:T(8,128)(2,1)} %get-tuple-element.133), calls=%async_computation | async-start | bytes 2097152 | tf_op jit(solution)/shard_map/all_to_all | solution.py:52
  21.5 4.2 %shard_map.159 = (bf16[2,16,2,8,128]{4,3,2,1,0:T(8,128)(2,1)}, bf16[2,16,2,8,128]{4,3,2,1,0:T(8,128)(2,1)}, bf16[2,16,2,8,128]{4,3,2,1,0:T(8,128)(2,1)}, bf16[2,...) custom-call(s32[1]{0:T(128)} %bitcast.1.place_ref.refs_0_, ...), custom_call_target="tpu_custom_call" | custom-call | tf_op jit(solution)/shard_map/pallas_call | solution.py:79
  26.1 1.6 collective-permute-start.1
  27.7 2.3 %collective-permute-start.2 = (bf16[2,16,2,8,128]{4,3,2,1,0:T(8,128)(2,1)}, bf16[2,16,2,8,128]{4,3,2,1,0:T(8,128)(2,1)S(1)}, u32[]{:S(2)}, u32[]{:S(2)}) collective-permute-start(bf16[2,16,2,8,128]{4,3,2,1,0:T(8,128)(2,1)} %get-tuple-element.103), channel_id=1, source_target_pairs={{0,3},{1,4},{2,5},{3,6},{4,7},{5,8},{6,9},{7,10},{8,11},{9,12},{10... | collective-permute-start | bytes 393224 | tf_op jit(solution)/shard_map/ppermute | solution.py:410
  30.0 1.5 collective-permute-start.3
  31.7 0.7 tile.10
  32.5 14.0 %collective-permute-done.refs_1_.refs_8_ = bf16[2,16,2,8,128]{4,3,2,1,0:T(8,128)(2,1)S(1)} collective-permute-done((bf16[2,16,2,8,128]{4,3,2,1,0:T(8,128)(2,1)}, bf16[2,16,2,8,128]{4,3,2,1,0:T(8,128)(2,1)S(1)}, u32[]{:S(2)}, u32[]{:S(2)}) %collective-permute-start) | collective-permute-done | bytes 131104 | tf_op jit(solution)/shard_map/ppermute | solution.py:410
  46.6 1.1 collective-permute-done.1.refs_2_.refs_9_
  47.7 4.7 %collective-permute-start.6 = (bf16[2,16,2,8,128]{4,3,2,1,0:T(8,128)(2,1)}, bf16[2,16,2,8,128]{4,3,2,1,0:T(8,128)(2,1)S(1)}, u32[]{:S(2)}, u32[]{:S(2)}) collective-permute-start(bf16[2,16,2,8,128]{4,3,2,1,0:T(8,128)(2,1)} %get-tuple-element.107), channel_id=1, source_target_pairs={{0,7},{1,8},{2,9},{3,10},{4,11},{5,12},{6,13},{7,14},{8,15},{9,0},... | collective-permute-start | bytes 393224 | tf_op jit(solution)/shard_map/ppermute | solution.py:410
  53.0 12.0 %collective-permute-start.8 = (bf16[2,16,2,8,128]{4,3,2,1,0:T(8,128)(2,1)}, bf16[2,16,2,8,128]{4,3,2,1,0:T(8,128)(2,1)S(1)}, u32[]{:S(2)}, u32[]{:S(2)}) collective-permute-start(bf16[2,16,2,8,128]{4,3,2,1,0:T(8,128)(2,1)} %get-tuple-element.109), channel_id=1, source_target_pairs={{0,9},{1,10},{2,11},{3,12},{4,13},{5,14},{6,15},{7,0},{8,1},{9,2},... | collective-permute-start | bytes 393224 | tf_op jit(solution)/shard_map/ppermute | solution.py:410
  65.0 8.6 %collective-permute-done.4.refs_5_.refs_12_ = bf16[2,16,2,8,128]{4,3,2,1,0:T(8,128)(2,1)S(1)} collective-permute-done((bf16[2,16,2,8,128]{4,3,2,1,0:T(8,128)(2,1)}, bf16[2,16,2,8,128]{4,3,2,1,0:T(8,128)(2,1)S(1)}, u32[]{:S(2)}, u32[]{:S(2)}) %collective-permute-start.4) | collective-permute-done | bytes 131104 | tf_op jit(solution)/shard_map/ppermute | solution.py:410
  73.9 0.9 collective-permute-done.5.refs_6_.refs_13_
  74.8 1.0 collective-permute-start.10
  75.8 7.1 %collective-permute-start.11 = (bf16[2,16,2,8,128]{4,3,2,1,0:T(8,128)(2,1)}, bf16[2,16,2,8,128]{4,3,2,1,0:T(8,128)(2,1)S(1)}, u32[]{:S(2)}, u32[]{:S(2)}) collective-permute-start(bf16[2,16,2,8,128]{4,3,2,1,0:T(8,128)(2,1)} %get-tuple-element.112), channel_id=1, source_target_pairs={{0,12},{1,13},{2,14},{3,15},{4,0},{5,1},{6,2},{7,3},{8,4},{9,5},{1... | collective-permute-start | bytes 393224 | tf_op jit(solution)/shard_map/ppermute | solution.py:410
  82.9 1.3 collective-permute-start.12
  84.2 4.8 %collective-permute-start.13 = (bf16[2,16,2,8,128]{4,3,2,1,0:T(8,128)(2,1)}, bf16[2,16,2,8,128]{4,3,2,1,0:T(8,128)(2,1)S(1)}, u32[]{:S(2)}, u32[]{:S(2)}) collective-permute-start(bf16[2,16,2,8,128]{4,3,2,1,0:T(8,128)(2,1)} %get-tuple-element.114), channel_id=1, source_target_pairs={{0,14},{1,15},{2,0},{3,1},{4,2},{5,3},{6,4},{7,5},{8,6},{9,7},{10,... | collective-permute-start | bytes 393224 | tf_op jit(solution)/shard_map/ppermute | solution.py:410
  89.0 3.1 %collective-permute-start.14 = (bf16[2,16,2,8,128]{4,3,2,1,0:T(8,128)(2,1)}, bf16[2,16,2,8,128]{4,3,2,1,0:T(8,128)(2,1)S(1)}, u32[]{:S(2)}, u32[]{:S(2)}) collective-permute-start(bf16[2,16,2,8,128]{4,3,2,1,0:T(8,128)(2,1)} %get-tuple-element.115), channel_id=1, source_target_pairs={{0,15},{1,0},{2,1},{3,2},{4,3},{5,4},{6,5},{7,6},{8,7},{9,8},{10,9... | collective-permute-start | bytes 393224 | tf_op jit(solution)/shard_map/ppermute | solution.py:410
  92.2 2.9 %collective-permute-done.13.refs_14_.refs_21_ = bf16[2,16,2,8,128]{4,3,2,1,0:T(8,128)(2,1)S(1)} collective-permute-done((bf16[2,16,2,8,128]{4,3,2,1,0:T(8,128)(2,1)}, bf16[2,16,2,8,128]{4,3,2,1,0:T(8,128)(2,1)S(1)}, u32[]{:S(2)}, u32[]{:S(2)}) %collective-permute-start.13) | collective-permute-done | bytes 131104 | tf_op jit(solution)/shard_map/ppermute | solution.py:410
  95.6 1.2 broadcast_in_dim.5
  96.8 1.1 collective-permute-start.15
  97.9 2.6 %collective-permute-start.16 = (bf16[16,16,128]{2,1,0:T(8,128)(2,1)}, bf16[16,16,128]{2,1,0:T(8,128)(2,1)S(1)}, u32[]{:S(2)}, u32[]{:S(2)}) collective-permute-start(bf16[16,16,128]{2,1,0:T(8,128)(2,1)} %get-tuple-element.136), channel_id=1, source_target_pairs={{0,2},{1,3},{2,4},{3,5},{4,6},{5,7},{6,8},{7,9},{8,10},{9,11},{10,... | collective-permute-start | bytes 196616 | tf_op jit(solution)/shard_map/ppermute | solution.py:410
  100.4 2.4 %collective-permute-start.19 = (bf16[16,16,128]{2,1,0:T(8,128)(2,1)}, bf16[16,16,128]{2,1,0:T(8,128)(2,1)S(1)}, u32[]{:S(2)}, u32[]{:S(2)}) collective-permute-start(bf16[16,16,128]{2,1,0:T(8,128)(2,1)} %get-tuple-element.139), channel_id=1, source_target_pairs={{0,5},{1,6},{2,7},{3,8},{4,9},{5,10},{6,11},{7,12},{8,13},{9,14},{... | collective-permute-start | bytes 196616 | tf_op jit(solution)/shard_map/ppermute | solution.py:410
  102.9 1.0 copy-done.1
  103.9 5.3 %shard_map.160 = bf16[16,2,24,128]{3,2,1,0:T(8,128)(2,1)} custom-call(s32[1]{0:T(128)} %bitcast.1.place_ref.refs_0_, f32[16,128,128]{2,1,0:T(8,128)} %bitcast.36, bf16[256,256]{1,0:T(8,128)(2,1)} %constant.35.clone.back_src.refs_2_, bf16[256,256]{1,0:T(8,128)(2,1)} %constant.33.clone.table_ref.fwd.refs_3_, bf16[256,256]{1,0:T(8,128)(2,1)} %constant.36.clone.back.refs_4_, ...), custom_call_target="tpu_custom_call" | custom-call | tf_op jit(solution)/shard_map/pallas_call | solution.py:235
  109.3 4.3 %all-to-all-start.1 = ((bf16[16,2,24,128]{3,2,1,0:T(8,128)(2,1)}), bf16[16,2,24,128]{3,2,1,0:T(8,128)(2,1)S(1)}, u32[]{:S(2)}, u32[]{:S(2)}) async-start(bf16[16,2,24,128]{3,2,1,0:T(8,128)(2,1)} %shard_map.160), calls=%async_computation.1 | async-start | bytes 393216 | tf_op jit(solution)/shard_map/all_to_all | solution.py:52
  113.6 2.9 %collective-permute-start.20 = (bf16[16,16,128]{2,1,0:T(8,128)(2,1)}, bf16[16,16,128]{2,1,0:T(8,128)(2,1)S(1)}, u32[]{:S(2)}, u32[]{:S(2)}) collective-permute-start(bf16[16,16,128]{2,1,0:T(8,128)(2,1)} %get-tuple-element.140), channel_id=1, source_target_pairs={{0,6},{1,7},{2,8},{3,9},{4,10},{5,11},{6,12},{7,13},{8,14},{9,15},... | collective-permute-start | bytes 196616 | tf_op jit(solution)/shard_map/ppermute | solution.py:410
  116.5 1.8 %collective-permute-start.21 = (bf16[16,16,128]{2,1,0:T(8,128)(2,1)}, bf16[16,16,128]{2,1,0:T(8,128)(2,1)S(1)}, u32[]{:S(2)}, u32[]{:S(2)}) collective-permute-start(bf16[16,16,128]{2,1,0:T(8,128)(2,1)} %get-tuple-element.141), channel_id=1, source_target_pairs={{0,7},{1,8},{2,9},{3,10},{4,11},{5,12},{6,13},{7,14},{8,15},{9,0},... | collective-permute-start | bytes 196616 | tf_op jit(solution)/shard_map/ppermute | solution.py:410
  118.3 0.6 collective-permute-start.22
  119.0 2.3 %collective-permute-start.23 = (bf16[16,16,128]{2,1,0:T(8,128)(2,1)}, bf16[16,16,128]{2,1,0:T(8,128)(2,1)S(1)}, u32[]{:S(2)}, u32[]{:S(2)}) collective-permute-start(bf16[16,16,128]{2,1,0:T(8,128)(2,1)} %get-tuple-element.143), channel_id=1, source_target_pairs={{0,9},{1,10},{2,11},{3,12},{4,13},{5,14},{6,15},{7,0},{8,1},{9,2},... | collective-permute-start | bytes 196616 | tf_op jit(solution)/shard_map/ppermute | solution.py:410
  121.2 1.5 collective-permute-start.24
  122.9 0.8 reshape.100.two_ref
  123.7 5.8 %collective-permute-done.20.refs_29_ = bf16[16,16,128]{2,1,0:T(8,128)(2,1)S(1)} collective-permute-done((bf16[16,16,128]{2,1,0:T(8,128)(2,1)}, bf16[16,16,128]{2,1,0:T(8,128)(2,1)S(1)}, u32[]{:S(2)}, u32[]{:S(2)}) %collective-permute-start.20) | collective-permute-done | bytes 65568 | tf_op jit(solution)/shard_map/ppermute | solution.py:410
  129.6 4.2 %collective-permute-start.26 = (bf16[16,16,128]{2,1,0:T(8,128)(2,1)}, bf16[16,16,128]{2,1,0:T(8,128)(2,1)S(1)}, u32[]{:S(2)}, u32[]{:S(2)}) collective-permute-start(bf16[16,16,128]{2,1,0:T(8,128)(2,1)} %get-tuple-element.146), channel_id=1, source_target_pairs={{0,12},{1,13},{2,14},{3,15},{4,0},{5,1},{6,2},{7,3},{8,4},{9,5},{1... | collective-permute-start | bytes 196616 | tf_op jit(solution)/shard_map/ppermute | solution.py:410
  133.8 0.8 collective-permute-start.27
  134.7 1.5 collective-permute-start.28
  136.1 1.0 collective-permute-start.29
  137.2 0.7 collective-permute-done.27.refs_36_
  137.9 1.4 collective-permute-done.28.refs_37_
  139.3 0.9 collective-permute-done.29.refs_38_
  141.0 5.3 %shard_map.161 = bf16[16,2,24,128]{3,2,1,0:T(8,128)(2,1)} custom-call(s32[1]{0:T(128)} %bitcast.1.place_ref.refs_0_, f32[16,128,128]{2,1,0:T(8,128)} %bitcast.37, bf16[256,256]{1,0:T(8,128)(2,1)} %constant.35.clone.back_src.refs_2_, bf16[256,256]{1,0:T(8,128)(2,1)} %constant.33.clone.table_ref.fwd.refs_3_, bf16[256,256]{1,0:T(8,128)(2,1)} %constant.36.clone.back.refs_4_, ...), custom_call_target="tpu_custom_call" | custom-call | tf_op jit(solution)/shard_map/pallas_call | solution.py:235
  146.3 6.1 %all-to-all-start.2 = ((bf16[16,2,24,128]{3,2,1,0:T(8,128)(2,1)}), bf16[16,2,24,128]{3,2,1,0:T(8,128)(2,1)S(1)}, u32[]{:S(2)}, u32[]{:S(2)}) async-start(bf16[16,2,24,128]{3,2,1,0:T(8,128)(2,1)} %shard_map.161), calls=%async_computation.2 | async-start | bytes 393216 | tf_op jit(solution)/shard_map/all_to_all | solution.py:52
  153.6 0.7 fusion.3.one_ref
  154.3 7.0 %all-to-all-done.2.wb_ref = bf16[16,2,24,128]{3,2,1,0:T(8,128)(2,1)S(1)} async-done(((bf16[16,2,24,128]{3,2,1,0:T(8,128)(2,1)}), bf16[16,2,24,128]{3,2,1,0:T(8,128)(2,1)S(1)}, u32[]{:S(2)}, u32[]{:S(2)}) %all-to-all-start.2) | async-done | bytes 196640 | tf_op jit(solution)/shard_map/all_to_all | solution.py:52
  161.3 0.7 copy-done.4
  162.0 12.2 %shard_map.162 = (f32[2,2,128,128]{3,2,1,0:T(8,128)}, f32[2,2,128,128]{3,2,1,0:T(8,128)}) custom-call(s32[2]{0:T(128)} %pad_add_fusion.base_ref, bf16[16,2,24,128]{3,2,1,0:T(8,128)(2,1)} %copy-done.3, bf16[16,2,24,128]{3,2,1,0:T(8,128)(2,1)} %copy-done.4, bf16[256,160]{1,0:T(8,128)(2,1)} %fusion.3.one_ref, bf16[48,768]{1,0:T(8,128)(2,1)} %reshape.100.two_ref, ...), custom_call_target="tpu_custom_call" | custom-call | tf_op jit(solution)/shard_map/pallas_call | solution.py:376
  (127 shorter events, 4.7 us)
Async XLA Ops:
  0.6 31.0 %copy-start = (bf16[27,64,2]{1,2,0:T(2,128)(2,1)S(1)}, bf16[27,64,2]{1,2,0:T(2,128)(2,1)}, u32[]{:S(2)}) copy-start(bf16[27,64,2]{1,2,0:T(2,128)(2,1)} %param.21) | copy-start | bytes 20740
  13.9 88.9 %all-to-all-start = ((bf16[16,16,16,128]{3,2,1,0:T(8,128)(2,1)}), bf16[16,16,16,128]{3,2,1,0:T(8,128)(2,1)S(1)}, u32[]{:S(2)}, u32[]{:S(2)}) async-start(bf16[16,16,16,128]{3,2,1,0:T(8,128)(2,1)} %get-tuple-element.133), calls=%async_computation | async-start | bytes 2097152 | tf_op jit(solution)/shard_map/all_to_all | solution.py:52
  21.5 70.6 %copy-start.35 = (bf16[27,2,64]{2,1,0:T(2,128)(2,1)S(1)}, bf16[27,2,64]{2,1,0:T(2,128)(2,1)}, u32[]{:S(2)}) copy-start(bf16[27,2,64]{2,1,0:T(2,128)(2,1)} %param.19) | copy-start | bytes 20740
  25.6 20.9 %collective-permute-start = (bf16[2,16,2,8,128]{4,3,2,1,0:T(8,128)(2,1)}, bf16[2,16,2,8,128]{4,3,2,1,0:T(8,128)(2,1)S(1)}, u32[]{:S(2)}, u32[]{:S(2)}) collective-permute-start(bf16[2,16,2,8,128]{4,3,2,1,0:T(8,128)(2,1)} %get-tuple-element.101), channel_id=1, source_target_pairs={{0,1},{1,2},{2,3},{3,4},{4,5},{5,6},{6,7},{7,8},{8,9},{9,10},{10,1... | collective-permute-start | bytes 393224 | tf_op jit(solution)/shard_map/ppermute | solution.py:410
  26.1 21.6 %collective-permute-start.1 = (bf16[2,16,2,8,128]{4,3,2,1,0:T(8,128)(2,1)}, bf16[2,16,2,8,128]{4,3,2,1,0:T(8,128)(2,1)S(1)}, u32[]{:S(2)}, u32[]{:S(2)}) collective-permute-start(bf16[2,16,2,8,128]{4,3,2,1,0:T(8,128)(2,1)} %get-tuple-element.102), channel_id=1, source_target_pairs={{0,2},{1,3},{2,4},{3,5},{4,6},{5,7},{6,8},{7,9},{8,10},{9,11},{10,... | collective-permute-start | bytes 393224 | tf_op jit(solution)/shard_map/ppermute | solution.py:410
  27.7 24.7 %collective-permute-start.2 = (bf16[2,16,2,8,128]{4,3,2,1,0:T(8,128)(2,1)}, bf16[2,16,2,8,128]{4,3,2,1,0:T(8,128)(2,1)S(1)}, u32[]{:S(2)}, u32[]{:S(2)}) collective-permute-start(bf16[2,16,2,8,128]{4,3,2,1,0:T(8,128)(2,1)} %get-tuple-element.103), channel_id=1, source_target_pairs={{0,3},{1,4},{2,5},{3,6},{4,7},{5,8},{6,9},{7,10},{8,11},{9,12},{10... | collective-permute-start | bytes 393224 | tf_op jit(solution)/shard_map/ppermute | solution.py:410
  30.0 23.0 %collective-permute-start.3 = (bf16[2,16,2,8,128]{4,3,2,1,0:T(8,128)(2,1)}, bf16[2,16,2,8,128]{4,3,2,1,0:T(8,128)(2,1)S(1)}, u32[]{:S(2)}, u32[]{:S(2)}) collective-permute-start(bf16[2,16,2,8,128]{4,3,2,1,0:T(8,128)(2,1)} %get-tuple-element.104), channel_id=1, source_target_pairs={{0,4},{1,5},{2,6},{3,7},{4,8},{5,9},{6,10},{7,11},{8,12},{9,13},{1... | collective-permute-start | bytes 393224 | tf_op jit(solution)/shard_map/ppermute | solution.py:410
  31.4 42.2 %collective-permute-start.4 = (bf16[2,16,2,8,128]{4,3,2,1,0:T(8,128)(2,1)}, bf16[2,16,2,8,128]{4,3,2,1,0:T(8,128)(2,1)S(1)}, u32[]{:S(2)}, u32[]{:S(2)}) collective-permute-start(bf16[2,16,2,8,128]{4,3,2,1,0:T(8,128)(2,1)} %get-tuple-element.105), channel_id=1, source_target_pairs={{0,5},{1,6},{2,7},{3,8},{4,9},{5,10},{6,11},{7,12},{8,13},{9,14},{... | collective-permute-start | bytes 393224 | tf_op jit(solution)/shard_map/ppermute | solution.py:410
  46.6 56.2 %copy-start.5 = (bf16[2,16,2,8,128]{4,3,2,1,0:T(8,128)(2,1)}, bf16[2,16,2,8,128]{4,3,2,1,0:T(8,128)(2,1)S(1)}, u32[]{:S(2)}) copy-start(bf16[2,16,2,8,128]{4,3,2,1,0:T(8,128)(2,1)S(1)} %collective-permute-done.refs_1_.refs_8_) | copy-start | bytes 393220
  46.6 28.2 %collective-permute-start.5 = (bf16[2,16,2,8,128]{4,3,2,1,0:T(8,128)(2,1)}, bf16[2,16,2,8,128]{4,3,2,1,0:T(8,128)(2,1)S(1)}, u32[]{:S(2)}, u32[]{:S(2)}) collective-permute-start(bf16[2,16,2,8,128]{4,3,2,1,0:T(8,128)(2,1)} %get-tuple-element.106), channel_id=1, source_target_pairs={{0,6},{1,7},{2,8},{3,9},{4,10},{5,11},{6,12},{7,13},{8,14},{9,15},... | collective-permute-start | bytes 393224 | tf_op jit(solution)/shard_map/ppermute | solution.py:410
  47.7 55.1 %copy-start.6 = (bf16[2,16,2,8,128]{4,3,2,1,0:T(8,128)(2,1)}, bf16[2,16,2,8,128]{4,3,2,1,0:T(8,128)(2,1)S(1)}, u32[]{:S(2)}) copy-start(bf16[2,16,2,8,128]{4,3,2,1,0:T(8,128)(2,1)S(1)} %collective-permute-done.1.refs_2_.refs_9_) | copy-start | bytes 393220
  47.7 28.1 %collective-permute-start.6 = (bf16[2,16,2,8,128]{4,3,2,1,0:T(8,128)(2,1)}, bf16[2,16,2,8,128]{4,3,2,1,0:T(8,128)(2,1)S(1)}, u32[]{:S(2)}, u32[]{:S(2)}) collective-permute-start(bf16[2,16,2,8,128]{4,3,2,1,0:T(8,128)(2,1)} %get-tuple-element.107), channel_id=1, source_target_pairs={{0,7},{1,8},{2,9},{3,10},{4,11},{5,12},{6,13},{7,14},{8,15},{9,0},... | collective-permute-start | bytes 393224 | tf_op jit(solution)/shard_map/ppermute | solution.py:410
  52.5 50.3 %copy-start.7 = (bf16[2,16,2,8,128]{4,3,2,1,0:T(8,128)(2,1)}, bf16[2,16,2,8,128]{4,3,2,1,0:T(8,128)(2,1)S(1)}, u32[]{:S(2)}) copy-start(bf16[2,16,2,8,128]{4,3,2,1,0:T(8,128)(2,1)S(1)} %collective-permute-done.2.refs_3_.refs_10_) | copy-start | bytes 393220
  52.5 30.5 %collective-permute-start.7 = (bf16[2,16,2,8,128]{4,3,2,1,0:T(8,128)(2,1)}, bf16[2,16,2,8,128]{4,3,2,1,0:T(8,128)(2,1)S(1)}, u32[]{:S(2)}, u32[]{:S(2)}) collective-permute-start(bf16[2,16,2,8,128]{4,3,2,1,0:T(8,128)(2,1)} %get-tuple-element.108), channel_id=1, source_target_pairs={{0,8},{1,9},{2,10},{3,11},{4,12},{5,13},{6,14},{7,15},{8,0},{9,1},... | collective-permute-start | bytes 393224 | tf_op jit(solution)/shard_map/ppermute | solution.py:410
  53.0 49.8 %copy-start.8 = (bf16[2,16,2,8,128]{4,3,2,1,0:T(8,128)(2,1)}, bf16[2,16,2,8,128]{4,3,2,1,0:T(8,128)(2,1)S(1)}, u32[]{:S(2)}) copy-start(bf16[2,16,2,8,128]{4,3,2,1,0:T(8,128)(2,1)S(1)} %collective-permute-done.3.refs_4_.refs_11_) | copy-start | bytes 393220
  53.0 31.2 %collective-permute-start.8 = (bf16[2,16,2,8,128]{4,3,2,1,0:T(8,128)(2,1)}, bf16[2,16,2,8,128]{4,3,2,1,0:T(8,128)(2,1)S(1)}, u32[]{:S(2)}, u32[]{:S(2)}) collective-permute-start(bf16[2,16,2,8,128]{4,3,2,1,0:T(8,128)(2,1)} %get-tuple-element.109), channel_id=1, source_target_pairs={{0,9},{1,10},{2,11},{3,12},{4,13},{5,14},{6,15},{7,0},{8,1},{9,2},... | collective-permute-start | bytes 393224 | tf_op jit(solution)/shard_map/ppermute | solution.py:410
  73.6 29.2 %copy-start.9 = (bf16[2,16,2,8,128]{4,3,2,1,0:T(8,128)(2,1)}, bf16[2,16,2,8,128]{4,3,2,1,0:T(8,128)(2,1)S(1)}, u32[]{:S(2)}) copy-start(bf16[2,16,2,8,128]{4,3,2,1,0:T(8,128)(2,1)S(1)} %collective-permute-done.4.refs_5_.refs_12_) | copy-start | bytes 393220
  73.6 15.4 %collective-permute-start.9 = (bf16[2,16,2,8,128]{4,3,2,1,0:T(8,128)(2,1)}, bf16[2,16,2,8,128]{4,3,2,1,0:T(8,128)(2,1)S(1)}, u32[]{:S(2)}, u32[]{:S(2)}) collective-permute-start(bf16[2,16,2,8,128]{4,3,2,1,0:T(8,128)(2,1)} %get-tuple-element.110), channel_id=1, source_target_pairs={{0,10},{1,11},{2,12},{3,13},{4,14},{5,15},{6,0},{7,1},{8,2},{9,3},... | collective-permute-start | bytes 393224 | tf_op jit(solution)/shard_map/ppermute | solution.py:410
  74.8 28.1 %copy-start.10 = (bf16[2,16,2,8,128]{4,3,2,1,0:T(8,128)(2,1)}, bf16[2,16,2,8,128]{4,3,2,1,0:T(8,128)(2,1)S(1)}, u32[]{:S(2)}) copy-start(bf16[2,16,2,8,128]{4,3,2,1,0:T(8,128)(2,1)S(1)} %collective-permute-done.5.refs_6_.refs_13_) | copy-start | bytes 393220
  74.8 17.4 %collective-permute-start.10 = (bf16[2,16,2,8,128]{4,3,2,1,0:T(8,128)(2,1)}, bf16[2,16,2,8,128]{4,3,2,1,0:T(8,128)(2,1)S(1)}, u32[]{:S(2)}, u32[]{:S(2)}) collective-permute-start(bf16[2,16,2,8,128]{4,3,2,1,0:T(8,128)(2,1)} %get-tuple-element.111), channel_id=1, source_target_pairs={{0,11},{1,12},{2,13},{3,14},{4,15},{5,0},{6,1},{7,2},{8,3},{9,4},{... | collective-permute-start | bytes 393224 | tf_op jit(solution)/shard_map/ppermute | solution.py:410
  75.8 27.0 %copy-start.11 = (bf16[2,16,2,8,128]{4,3,2,1,0:T(8,128)(2,1)}, bf16[2,16,2,8,128]{4,3,2,1,0:T(8,128)(2,1)S(1)}, u32[]{:S(2)}) copy-start(bf16[2,16,2,8,128]{4,3,2,1,0:T(8,128)(2,1)S(1)} %collective-permute-done.6.refs_7_.refs_14_) | copy-start | bytes 393220
  75.8 16.4 %collective-permute-start.11 = (bf16[2,16,2,8,128]{4,3,2,1,0:T(8,128)(2,1)}, bf16[2,16,2,8,128]{4,3,2,1,0:T(8,128)(2,1)S(1)}, u32[]{:S(2)}, u32[]{:S(2)}) collective-permute-start(bf16[2,16,2,8,128]{4,3,2,1,0:T(8,128)(2,1)} %get-tuple-element.112), channel_id=1, source_target_pairs={{0,12},{1,13},{2,14},{3,15},{4,0},{5,1},{6,2},{7,3},{8,4},{9,5},{1... | collective-permute-start | bytes 393224 | tf_op jit(solution)/shard_map/ppermute | solution.py:410
  82.9 19.9 %copy-start.12 = (bf16[2,16,2,8,128]{4,3,2,1,0:T(8,128)(2,1)}, bf16[2,16,2,8,128]{4,3,2,1,0:T(8,128)(2,1)S(1)}, u32[]{:S(2)}) copy-start(bf16[2,16,2,8,128]{4,3,2,1,0:T(8,128)(2,1)S(1)} %collective-permute-done.7.refs_8_.refs_15_) | copy-start | bytes 393220
  82.9 9.3 %collective-permute-start.12 = (bf16[2,16,2,8,128]{4,3,2,1,0:T(8,128)(2,1)}, bf16[2,16,2,8,128]{4,3,2,1,0:T(8,128)(2,1)S(1)}, u32[]{:S(2)}, u32[]{:S(2)}) collective-permute-start(bf16[2,16,2,8,128]{4,3,2,1,0:T(8,128)(2,1)} %get-tuple-element.113), channel_id=1, source_target_pairs={{0,13},{1,14},{2,15},{3,0},{4,1},{5,2},{6,3},{7,4},{8,5},{9,6},{10... | collective-permute-start | bytes 393224 | tf_op jit(solution)/shard_map/ppermute | solution.py:410
  84.2 10.9 %collective-permute-start.13 = (bf16[2,16,2,8,128]{4,3,2,1,0:T(8,128)(2,1)}, bf16[2,16,2,8,128]{4,3,2,1,0:T(8,128)(2,1)S(1)}, u32[]{:S(2)}, u32[]{:S(2)}) collective-permute-start(bf16[2,16,2,8,128]{4,3,2,1,0:T(8,128)(2,1)} %get-tuple-element.114), channel_id=1, source_target_pairs={{0,14},{1,15},{2,0},{3,1},{4,2},{5,3},{6,4},{7,5},{8,6},{9,7},{10,... | collective-permute-start | bytes 393224 | tf_op jit(solution)/shard_map/ppermute | solution.py:410
  89.0 6.6 %collective-permute-start.14 = (bf16[2,16,2,8,128]{4,3,2,1,0:T(8,128)(2,1)}, bf16[2,16,2,8,128]{4,3,2,1,0:T(8,128)(2,1)S(1)}, u32[]{:S(2)}, u32[]{:S(2)}) collective-permute-start(bf16[2,16,2,8,128]{4,3,2,1,0:T(8,128)(2,1)} %get-tuple-element.115), channel_id=1, source_target_pairs={{0,15},{1,0},{2,1},{3,2},{4,3},{5,4},{6,5},{7,6},{8,7},{9,8},{10,9... | collective-permute-start | bytes 393224 | tf_op jit(solution)/shard_map/ppermute | solution.py:410
  96.8 16.8 %collective-permute-start.15 = (bf16[16,16,128]{2,1,0:T(8,128)(2,1)}, bf16[16,16,128]{2,1,0:T(8,128)(2,1)S(1)}, u32[]{:S(2)}, u32[]{:S(2)}) collective-permute-start(bf16[16,16,128]{2,1,0:T(8,128)(2,1)} %get-tuple-element.135), channel_id=1, source_target_pairs={{0,1},{1,2},{2,3},{3,4},{4,5},{5,6},{6,7},{7,8},{8,9},{9,10},{10,1... | collective-permute-start | bytes 196616 | tf_op jit(solution)/shard_map/ppermute | solution.py:410
  97.9 18.6 %collective-permute-start.16 = (bf16[16,16,128]{2,1,0:T(8,128)(2,1)}, bf16[16,16,128]{2,1,0:T(8,128)(2,1)S(1)}, u32[]{:S(2)}, u32[]{:S(2)}) collective-permute-start(bf16[16,16,128]{2,1,0:T(8,128)(2,1)} %get-tuple-element.136), channel_id=1, source_target_pairs={{0,2},{1,3},{2,4},{3,5},{4,6},{5,7},{6,8},{7,9},{8,10},{9,11},{10,... | collective-permute-start | bytes 196616 | tf_op jit(solution)/shard_map/ppermute | solution.py:410
  100.4 17.9 %collective-permute-start.17 = (bf16[16,16,128]{2,1,0:T(8,128)(2,1)}, bf16[16,16,128]{2,1,0:T(8,128)(2,1)S(1)}, u32[]{:S(2)}, u32[]{:S(2)}) collective-permute-start(bf16[16,16,128]{2,1,0:T(8,128)(2,1)} %get-tuple-element.137), channel_id=1, source_target_pairs={{0,3},{1,4},{2,5},{3,6},{4,7},{5,8},{6,9},{7,10},{8,11},{9,12},{10... | collective-permute-start | bytes 196616 | tf_op jit(solution)/shard_map/ppermute | solution.py:410
  100.4 18.5 %collective-permute-start.18 = (bf16[16,16,128]{2,1,0:T(8,128)(2,1)}, bf16[16,16,128]{2,1,0:T(8,128)(2,1)S(1)}, u32[]{:S(2)}, u32[]{:S(2)}) collective-permute-start(bf16[16,16,128]{2,1,0:T(8,128)(2,1)} %get-tuple-element.138), channel_id=1, source_target_pairs={{0,4},{1,5},{2,6},{3,7},{4,8},{5,9},{6,10},{7,11},{8,12},{9,13},{1... | collective-permute-start | bytes 196616 | tf_op jit(solution)/shard_map/ppermute | solution.py:410
  100.4 20.8 %collective-permute-start.19 = (bf16[16,16,128]{2,1,0:T(8,128)(2,1)}, bf16[16,16,128]{2,1,0:T(8,128)(2,1)S(1)}, u32[]{:S(2)}, u32[]{:S(2)}) collective-permute-start(bf16[16,16,128]{2,1,0:T(8,128)(2,1)} %get-tuple-element.139), channel_id=1, source_target_pairs={{0,5},{1,6},{2,7},{3,8},{4,9},{5,10},{6,11},{7,12},{8,13},{9,14},{... | collective-permute-start | bytes 196616 | tf_op jit(solution)/shard_map/ppermute | solution.py:410
  109.3 37.0 %all-to-all-start.1 = ((bf16[16,2,24,128]{3,2,1,0:T(8,128)(2,1)}), bf16[16,2,24,128]{3,2,1,0:T(8,128)(2,1)S(1)}, u32[]{:S(2)}, u32[]{:S(2)}) async-start(bf16[16,2,24,128]{3,2,1,0:T(8,128)(2,1)} %shard_map.160), calls=%async_computation.1 | async-start | bytes 393216 | tf_op jit(solution)/shard_map/all_to_all | solution.py:52
  113.6 26.6 %copy-start.20 = (bf16[16,16,128]{2,1,0:T(8,128)(2,1)}, bf16[16,16,128]{2,1,0:T(8,128)(2,1)S(1)}, u32[]{:S(2)}) copy-start(bf16[16,16,128]{2,1,0:T(8,128)(2,1)S(1)} %collective-permute-done.15.refs_24_) | copy-start | bytes 196612
  113.6 15.9 %collective-permute-start.20 = (bf16[16,16,128]{2,1,0:T(8,128)(2,1)}, bf16[16,16,128]{2,1,0:T(8,128)(2,1)S(1)}, u32[]{:S(2)}, u32[]{:S(2)}) collective-permute-start(bf16[16,16,128]{2,1,0:T(8,128)(2,1)} %get-tuple-element.140), channel_id=1, source_target_pairs={{0,6},{1,7},{2,8},{3,9},{4,10},{5,11},{6,12},{7,13},{8,14},{9,15},... | collective-permute-start | bytes 196616 | tf_op jit(solution)/shard_map/ppermute | solution.py:410
  116.5 23.7 %copy-start.21 = (bf16[16,16,128]{2,1,0:T(8,128)(2,1)}, bf16[16,16,128]{2,1,0:T(8,128)(2,1)S(1)}, u32[]{:S(2)}) copy-start(bf16[16,16,128]{2,1,0:T(8,128)(2,1)S(1)} %collective-permute-done.16.refs_25_) | copy-start | bytes 196612
  116.5 13.1 %collective-permute-start.21 = (bf16[16,16,128]{2,1,0:T(8,128)(2,1)}, bf16[16,16,128]{2,1,0:T(8,128)(2,1)S(1)}, u32[]{:S(2)}, u32[]{:S(2)}) collective-permute-start(bf16[16,16,128]{2,1,0:T(8,128)(2,1)} %get-tuple-element.141), channel_id=1, source_target_pairs={{0,7},{1,8},{2,9},{3,10},{4,11},{5,12},{6,13},{7,14},{8,15},{9,0},... | collective-permute-start | bytes 196616 | tf_op jit(solution)/shard_map/ppermute | solution.py:410
  118.3 21.9 %copy-start.22 = (bf16[16,16,128]{2,1,0:T(8,128)(2,1)}, bf16[16,16,128]{2,1,0:T(8,128)(2,1)S(1)}, u32[]{:S(2)}) copy-start(bf16[16,16,128]{2,1,0:T(8,128)(2,1)S(1)} %collective-permute-done.17.refs_26_) | copy-start | bytes 196612
  118.3 15.5 %collective-permute-start.22 = (bf16[16,16,128]{2,1,0:T(8,128)(2,1)}, bf16[16,16,128]{2,1,0:T(8,128)(2,1)S(1)}, u32[]{:S(2)}, u32[]{:S(2)}) collective-permute-start(bf16[16,16,128]{2,1,0:T(8,128)(2,1)} %get-tuple-element.142), channel_id=1, source_target_pairs={{0,8},{1,9},{2,10},{3,11},{4,12},{5,13},{6,14},{7,15},{8,0},{9,1},... | collective-permute-start | bytes 196616 | tf_op jit(solution)/shard_map/ppermute | solution.py:410
  119.0 21.3 %copy-start.23 = (bf16[16,16,128]{2,1,0:T(8,128)(2,1)}, bf16[16,16,128]{2,1,0:T(8,128)(2,1)S(1)}, u32[]{:S(2)}) copy-start(bf16[16,16,128]{2,1,0:T(8,128)(2,1)S(1)} %collective-permute-done.18.refs_27_) | copy-start | bytes 196612
  119.0 15.7 %collective-permute-start.23 = (bf16[16,16,128]{2,1,0:T(8,128)(2,1)}, bf16[16,16,128]{2,1,0:T(8,128)(2,1)S(1)}, u32[]{:S(2)}, u32[]{:S(2)}) collective-permute-start(bf16[16,16,128]{2,1,0:T(8,128)(2,1)} %get-tuple-element.143), channel_id=1, source_target_pairs={{0,9},{1,10},{2,11},{3,12},{4,13},{5,14},{6,15},{7,0},{8,1},{9,2},... | collective-permute-start | bytes 196616 | tf_op jit(solution)/shard_map/ppermute | solution.py:410
  121.2 19.0 %copy-start.24 = (bf16[16,16,128]{2,1,0:T(8,128)(2,1)}, bf16[16,16,128]{2,1,0:T(8,128)(2,1)S(1)}, u32[]{:S(2)}) copy-start(bf16[16,16,128]{2,1,0:T(8,128)(2,1)S(1)} %collective-permute-done.19.refs_28_) | copy-start | bytes 196612
  121.2 14.9 %collective-permute-start.24 = (bf16[16,16,128]{2,1,0:T(8,128)(2,1)}, bf16[16,16,128]{2,1,0:T(8,128)(2,1)S(1)}, u32[]{:S(2)}, u32[]{:S(2)}) collective-permute-start(bf16[16,16,128]{2,1,0:T(8,128)(2,1)} %get-tuple-element.144), channel_id=1, source_target_pairs={{0,10},{1,11},{2,12},{3,13},{4,14},{5,15},{6,0},{7,1},{8,2},{9,3},... | collective-permute-start | bytes 196616 | tf_op jit(solution)/shard_map/ppermute | solution.py:410
  129.6 7.6 %collective-permute-start.25 = (bf16[16,16,128]{2,1,0:T(8,128)(2,1)}, bf16[16,16,128]{2,1,0:T(8,128)(2,1)S(1)}, u32[]{:S(2)}, u32[]{:S(2)}) collective-permute-start(bf16[16,16,128]{2,1,0:T(8,128)(2,1)} %get-tuple-element.145), channel_id=1, source_target_pairs={{0,11},{1,12},{2,13},{3,14},{4,15},{5,0},{6,1},{7,2},{8,3},{9,4},{... | collective-permute-start | bytes 196616 | tf_op jit(solution)/shard_map/ppermute | solution.py:410
  129.6 7.5 %collective-permute-start.26 = (bf16[16,16,128]{2,1,0:T(8,128)(2,1)}, bf16[16,16,128]{2,1,0:T(8,128)(2,1)S(1)}, u32[]{:S(2)}, u32[]{:S(2)}) collective-permute-start(bf16[16,16,128]{2,1,0:T(8,128)(2,1)} %get-tuple-element.146), channel_id=1, source_target_pairs={{0,12},{1,13},{2,14},{3,15},{4,0},{5,1},{6,2},{7,3},{8,4},{9,5},{1... | collective-permute-start | bytes 196616 | tf_op jit(solution)/shard_map/ppermute | solution.py:410
  133.8 4.1 %collective-permute-start.27 = (bf16[16,16,128]{2,1,0:T(8,128)(2,1)}, bf16[16,16,128]{2,1,0:T(8,128)(2,1)S(1)}, u32[]{:S(2)}, u32[]{:S(2)}) collective-permute-start(bf16[16,16,128]{2,1,0:T(8,128)(2,1)} %get-tuple-element.147), channel_id=1, source_target_pairs={{0,13},{1,14},{2,15},{3,0},{4,1},{5,2},{6,3},{7,4},{8,5},{9,6},{10... | collective-permute-start | bytes 196616 | tf_op jit(solution)/shard_map/ppermute | solution.py:410
  134.7 4.6 %collective-permute-start.28 = (bf16[16,16,128]{2,1,0:T(8,128)(2,1)}, bf16[16,16,128]{2,1,0:T(8,128)(2,1)S(1)}, u32[]{:S(2)}, u32[]{:S(2)}) collective-permute-start(bf16[16,16,128]{2,1,0:T(8,128)(2,1)} %get-tuple-element.148), channel_id=1, source_target_pairs={{0,14},{1,15},{2,0},{3,1},{4,2},{5,3},{6,4},{7,5},{8,6},{9,7},{10,... | collective-permute-start | bytes 196616 | tf_op jit(solution)/shard_map/ppermute | solution.py:410
  136.1 4.1 %collective-permute-start.29 = (bf16[16,16,128]{2,1,0:T(8,128)(2,1)}, bf16[16,16,128]{2,1,0:T(8,128)(2,1)S(1)}, u32[]{:S(2)}, u32[]{:S(2)}) collective-permute-start(bf16[16,16,128]{2,1,0:T(8,128)(2,1)} %get-tuple-element.149), channel_id=1, source_target_pairs={{0,15},{1,0},{2,1},{3,2},{4,3},{5,4},{6,5},{7,6},{8,7},{9,8},{10,9... | collective-permute-start | bytes 196616 | tf_op jit(solution)/shard_map/ppermute | solution.py:410
  146.3 15.0 %all-to-all-start.2 = ((bf16[16,2,24,128]{3,2,1,0:T(8,128)(2,1)}), bf16[16,2,24,128]{3,2,1,0:T(8,128)(2,1)S(1)}, u32[]{:S(2)}, u32[]{:S(2)}) async-start(bf16[16,2,24,128]{3,2,1,0:T(8,128)(2,1)} %shard_map.161), calls=%async_computation.2 | async-start | bytes 393216 | tf_op jit(solution)/shard_map/all_to_all | solution.py:52
  (24 other events, 214.3 us)
where the time goes:
time: 175 us; the launch traced here: 174 us
  starting transfers between devices  81 us (46%)
  waiting for transfers between devices  44 us (25%)
  Pallas kernels  38.3 us (22%)
  local copies, waits for them, and re-layouts  6.53 us (4%)
  other arithmetic  2.52 us (1%)
    ppermute x30, starting transfers between devices, send(): lax.ppermute(blocks[k], 'slc', [(i, (i + k) % n) for i in range(n)])  63.1 us
    ppermute x30, waiting for transfers between devices, send(): lax.ppermute(blocks[k], 'slc', [(i, (i + k) % n) for i in range(n)])  37 us
    all_to_all x3, starting transfers between devices, swap(): lax.all_to_all(blocks, 'slc', split_axis=0, concat_axis=0, tiled=True)  17.9 us
    pallas_call x1, Pallas kernels, denoise(): pl.pallas_call(denoise_kernel, out_shape=(shape, shape), in_specs=[SMEM,...  12.2 us
    pallas_call x1, Pallas kernels, point_step(): pl.pallas_call(point_kernel, out_shape=[jax.ShapeDtypeStruct((n, *block),...  11.3 us
    pallas_call x2, Pallas kernels, data_step(): pl.pallas_call(kernel, out_shape=jax.ShapeDtypeStruct((n, 2, depth_cols +...  10.7 us
    all_to_all x3, waiting for transfers between devices, swap(): lax.all_to_all(blocks, 'slc', split_axis=0, concat_axis=0, tiled=True)  7.01 us
    pallas_call x1, Pallas kernels, maps_step(): pl.pallas_call(maps_kernel, grid=(coils // MAPS_AT_ONCE,), out_shape=[jax...  4.16 us
  transfers between devices with their start and end apart: 33, of which 12 were waited for; matrix products, arithmetic and copies ran while one was open for 3% of the time, Pallas kernels for 9%

commit v1 on v0

--- a/solution.py
+++ b/solution.py
@@ -64,11 +64,16 @@
     for c in range(coils):
         for p in range(2):
             turned = [
-                jnp.transpose(m_ref[p, z, c]).astype(FULL).reshape(n, SETS * part, H) for z in range(depth)
+                jnp.transpose(m_ref[p, z, c]).astype(FULL).reshape(SETS, n // 2, 2 * part, H)
+                for z in range(depth)
             ]
             for i in range(SETS):
-                rows = [t[:, i * part : (i + 1) * part] for t in turned]
-                scratch[:, i, c, p] = jnp.concatenate(rows, axis=1).astype(LOW)
+                sides = [
+                    jnp.concatenate([t[i, :, side * part : (side + 1) * part] for t in turned], axis=1)
+                    for side in range(2)
+                ]
+                both = jnp.stack(sides, axis=1).reshape(n, depth * part, H)
+                scratch[:, i, c, p] = both.astype(LOW)
     for k in range(n):
         outs[k][...] = scratch[lax.rem(place_ref[0] + k, n)]
 
@@ -269,26 +274,29 @@
     return sent.transpose(0, 1, 3, 2, 4)
 
 
-def denoise_kernel(base_ref, wa_ref, wb_ref, one_ref, two_ref, last_ref, est_ref, dual_ref, cols, acc):
-    blocks, _, tall, L = wa_ref.shape
+def gather_rows(refs, i, z, part):
+    pieces = []
+    for ref, skip in refs:
+        count = ref.shape[0]
+        pairs = ref[skip:, i].astype(FULL).reshape((count - skip) // 2, 2, *ref.shape[2:])
+        sides = [pairs[:, side, z * part : (z + 1) * part] for side in range(2)]
+        pieces.append(jnp.concatenate(sides, axis=1).reshape(-1, ref.shape[-1]))
+    return jnp.concatenate(pieces, axis=0) if len(pieces) > 1 else pieces[0]
+
+
+def hidden_blocks(base_ref, refs, one_ref, two_ref, acc, cols, start):
     part = GROUP // SETS
-    window = tall // part
+    window, blocks = cols.shape[1], cols.shape[3]
+    L = cols.shape[-1]
     R = blocks * GROUP
-    depth = window - 4
     slices = base_ref[1]
     lane = lax.broadcasted_iota(jnp.int32, (R, L), 1)
     row = lax.broadcasted_iota(jnp.int32, (R, L), 0)
 
-    def field(i, z):
-        both = [
-            ref[:, i].astype(FULL)[:, z * part : (z + 1) * part] for ref in (wa_ref, wb_ref)
-        ]
-        return jnp.concatenate(both, axis=1).reshape(R, L)
-
     for z in range(window):
         moved = ([], [])
         for i in range(2):
-            f = field(i, z)
+            f = gather_rows(refs, i, z, part)
             moved[0].append(jnp.where(row < 2, 0.0, pltpu.roll(f, 2, axis=0)))
             moved[1].append(jnp.where(row >= R - 2, 0.0, pltpu.roll(f, R - 2, axis=0)))
         for phase in range(2):
@@ -311,13 +319,13 @@
 
     first_live, last_live = live(0), live(window - 3)
 
-    @pl.loop(0, blocks)
+    @pl.loop(0, acc.shape[3])
     def _(j):
         for phase in range(2):
 
             def gathered(k):
                 return jnp.concatenate(
-                    [cols[phase, k + a, b, j] for a in range(3) for b in range(3)], axis=0
+                    [cols[phase, k + a, b, start + j] for a in range(3) for b in range(3)], axis=0
                 )
 
             hidden = []
@@ -327,13 +335,12 @@
                 hidden.append(jnp.maximum(summed, 0.0))
             edge = [(hidden[0][:, :L] * first_live).astype(LOW), (hidden[1][:, L:] * last_live).astype(LOW)]
             inner = [hidden[0][:, L:].astype(LOW), hidden[1][:, :L].astype(LOW)]
-            hidden = [
-                jnp.concatenate([edge[0], inner[0]], axis=1),
-                jnp.concatenate([inner[1], edge[1]], axis=1),
+            stacked = [
+                jnp.concatenate(pair, axis=1)
+                for pair in ((edge[0], inner[0]), (inner[0], inner[1]), (inner[1], edge[1]))
             ]
+            terms = matmul(two_ref[...], jnp.concatenate(stacked, axis=0))
             width = 2 * GROUP
-            middle = jnp.concatenate([inner[0], inner[1]], axis=1)
-            terms = matmul(two_ref[...], jnp.concatenate([hidden[0], middle, hidden[1]], axis=0))
             for z in range(2):
                 left, mid, right = [
                     terms[i * width : (i + 1) * width, z * L : (z + 1) * L] for i in range(3)
@@ -344,20 +351,32 @@
                 for o in range(2):
                     acc[phase, z, o, j] = both[o * GROUP : (o + 1) * GROUP]
 
+
+def near_kernel(base_ref, wa_ref, one_ref, two_ref, acc, cols):
+    hidden_blocks(base_ref, [(wa_ref, 0)], one_ref, two_ref, acc, cols, 0)
+
+
+def far_kernel(base_ref, wa_ref, wb_ref, near_ref, one_ref, two_ref, last_ref, est_ref, dual_ref, cols, acc):
+    part = GROUP // SETS
+    overlap = cols.shape[3] * GROUP - wb_ref.shape[0] * part
+    skip = wa_ref.shape[0] - overlap // part
+    hidden_blocks(base_ref, [(wa_ref, skip), (wb_ref, 0)], one_ref, two_ref, acc, cols, cols.shape[3] - acc.shape[3])
+    _, depth, L, R = est_ref.shape
+    row = lax.broadcasted_iota(jnp.int32, (R, L), 0)
     for z in range(depth):
         for o in range(2):
-            even = pltpu.roll(acc[0, z, o].reshape(R, L), R - 2, axis=0)
-            odd = pltpu.roll(acc[1, z, o].reshape(R, L), 2, axis=0)
-            noise = jnp.where(row >= R - 2, 0.0, even) + jnp.where(row < 2, 0.0, odd) + last_ref[o]
-            est_ref[o, z] = jnp.transpose(field(o, z + 2) - noise)
+            even, odd = [
+                jnp.concatenate([ref[phase, z, o] for ref in (near_ref, acc)], axis=0).reshape(R, L)
+                for phase in range(2)
+            ]
+            even = jnp.where(row >= R - 2, 0.0, pltpu.roll(even, R - 2, axis=0))
+            odd = jnp.where(row < 2, 0.0, pltpu.roll(odd, 2, axis=0))
+            noise = even + odd + last_ref[o]
+            est_ref[o, z] = jnp.transpose(gather_rows([(wa_ref, 0), (wb_ref, 0)], o, z + 2, part) - noise)
             dual_ref[o, z] = jnp.transpose(noise)
 
 
-def denoise(base, windows, one, bias, two, last):
-    blocks, _, tall, L = windows[0].shape
-    spread = tall * SETS // GROUP
-    depth = spread - 4
-    R = blocks * GROUP
+def denoise_weights(one, bias, two):
     taps_one = one.reshape(3, 3, 3, 2, -1)
     taps_two = two.reshape(3, 3, 3, -1, 2)
     hid = taps_one.shape[-1]
@@ -372,17 +391,38 @@
         left = left - terms[-1]
     terms = jnp.stack(terms, axis=1).astype(LOW)
     first = jnp.concatenate([first, jnp.pad(terms, ((0, 0), (0, 2 * GROUP - 3)))], axis=1)
-    shape = jax.ShapeDtypeStruct((2, depth, L, R), FULL)
+    return first, second
+
+
+def denoise_near(base, window, first, second):
+    count, _, tall, L = window.shape
+    spread = tall * SETS // GROUP
+    blocks = count * GROUP // SETS // GROUP
     return pl.pallas_call(
-        denoise_kernel,
+        near_kernel,
+        out_shape=jax.ShapeDtypeStruct((2, spread - 4, 2, blocks - 1, GROUP, L), FULL),
+        in_specs=[SMEM, VMEM, VMEM, VMEM],
+        out_specs=VMEM,
+        scratch_shapes=[pltpu.VMEM((2, spread, 3, blocks, 2 * GROUP, L), LOW)],
+    )(base, window, first, second)
+
+
+def denoise_far(base, windows, near, first, second, last):
+    count, _, tall, L = windows[0].shape
+    spread = tall * SETS // GROUP
+    depth = spread - 4
+    half = count * GROUP // SETS // GROUP
+    shape = jax.ShapeDtypeStruct((2, depth, L, 2 * half * GROUP), FULL)
+    return pl.pallas_call(
+        far_kernel,
         out_shape=(shape, shape),
-        in_specs=[SMEM, VMEM, VMEM, VMEM, VMEM, SMEM],
+        in_specs=[SMEM] + [VMEM] * 5 + [SMEM],
         out_specs=(VMEM, VMEM),
         scratch_shapes=[
-            pltpu.VMEM((2, spread, 3, blocks, 2 * GROUP, L), LOW),
-            pltpu.VMEM((2, depth, 2, blocks, GROUP, L), FULL),
+            pltpu.VMEM((2, spread, 3, half + 2, 2 * GROUP, L), LOW),
+            pltpu.VMEM((2, depth, 2, half + 1, GROUP, L), FULL),
         ],
-    )(base, *windows, first, second, last)
+    )(base, *windows, near, first, second, last)
 
 
 def on_device(
@@ -395,6 +435,10 @@
     lines = points // W
     ncol = W // n
 
+    base = jnp.stack([position * depth, jnp.int32(slices)]).astype(jnp.int32)
+    weights = denoise_weights(
+        tap_kernel(tap_order, first_kernel), first_bias, tap_kernel(tap_order, second_kernel)
+    )
     fits = ncol == GROUP and coils * lines == W and coils % AT_ONCE == 0
     table_f, table_g = make_table(H, -1.0), make_table(H, 1.0)
     depth_f, depth_g = make_table(slices, -1.0), make_table(slices, 1.0)
@@ -404,19 +448,22 @@
         part = ncol // SETS
         place = position.astype(jnp.int32)[None]
 
+        order = sorted(range(1, n), key=lambda k: abs(2 * k - n))
+
         def send(blocks):
             got = list(blocks)
-            for k in sorted(range(1, n), key=lambda k: abs(2 * k - n)):
+            for k in order:
                 got[k] = lax.ppermute(blocks[k], "slc", [(i, (i + k) % n) for i in range(n)])
             return got
 
         maps = maps_step(place, coil_maps, n)
         maps = send(maps)
         own_mask = own_mask.transpose(0, 2, 1).reshape(slices, lines * coils).astype(FULL)
-        table_x = make_table(W, 1.0).reshape(2 * W, 2 * W)
+        table_rows = make_table(W, 1.0).reshape(2 * W, 2, SETS, n, part)
+        table_rows = table_rows.transpose(1, 3, 2, 4, 0).reshape(2 * W, 2 * W)
         depth_t = spread_table(depth_g, ncol).T
         depth_t = depth_t.reshape(-1, 2, slices, SETS, part).transpose(0, 3, 1, 2, 4).reshape(depth_t.shape)
-        by_z = point_step(place, kspace, own_mask, low(table_x.T), low(depth_t), n)
+        by_z = point_step(place, kspace, own_mask, low(table_rows), low(depth_t), n)
         back_src = table_g.reshape(2, n, lines, 2 * H).transpose(1, 0, 2, 3).reshape(2 * H, 2 * H)
         tables = [
             low(table)
@@ -431,7 +478,12 @@
         tall_mask = jnp.repeat(mask, part, axis=1)
         first = by_z[0]
         first = [swap(first)]
-        later, tall_mask, maps = lax.optimization_barrier((by_z[1:], tall_mask, maps))
+        held = [maps[k] for k in order[: n - 3]]
+        later, tall_mask, held, base, weights = lax.optimization_barrier(
+            (by_z[1:], tall_mask, held, base, weights)
+        )
+        for k, block in zip(order[: n - 3], held):
+            maps[k] = block
         later = send(later)
         windows = []
         for i, spectra in enumerate((first, later)):
@@ -448,14 +500,13 @@
         by_z = by_z.reshape(n, ncol, coils, 2 * lines, slices).transpose(0, 2, 3, 4, 1)
         spectra = swap(by_z.reshape(n, coils, 2 * lines, slices * ncol))
         got = swap(data_step_plain(maps, spectra, mask, *map(low, (table_f, table_g, depth_f, depth_g))))
-        got = got.transpose(0, 3, 1, 2, 4).reshape(W // GROUP, SETS, GROUP // SETS, 2, depth + 4, H)
-        got = got.transpose(1, 0, 3, 4, 2, 5).reshape(SETS, W // GROUP, 2, -1, H)
+        part = GROUP // SETS
+        got = got.transpose(0, 3, 1, 2, 4).reshape(SETS, W // GROUP, part, 2, depth + 4, H)
+        got = got.transpose(0, 1, 3, 4, 2, 5).reshape(SETS, W // GROUP, 2, -1, H)
         windows = [got[i] for i in range(SETS)]
 
-    kernel_one = tap_kernel(tap_order, first_kernel)
-    kernel_two = tap_kernel(tap_order, second_kernel)
-    base = jnp.stack([position * depth, jnp.int32(slices)]).astype(jnp.int32)
-    return denoise(base, windows, kernel_one, first_bias, kernel_two, second_bias)
+    near = denoise_near(base, windows[0], *weights)
+    return denoise_far(base, windows, near, *weights, second_bias)
 
 
 def solution(mesh):

time: 175 us -> 171 us (0.977)
  starting transfers between devices: 81 us -> 66.6 us
  waiting for transfers between devices: 44 us -> 52.9 us
  Pallas kernels: 38.3 us -> 40.3 us
    ppermute x30, starting transfers between devices: 63.1 us -> 49.1 us  [send(): lax.ppermute(blocks[k], 'slc', [(i, (i + k) % n) for i in range(n)])]
    ppermute x30, waiting for transfers between devices: 37 us -> 50.2 us  [send(): lax.ppermute(blocks[k], 'slc', [(i, (i + k) % n) for i in range(n)])]
    all_to_all x3, waiting for transfers between devices: 7.01 us -> 2.76 us  [swap(): lax.all_to_all(blocks, 'slc', split_axis=0, concat_axis=0, tiled=True)]
    pallas_call x1 -> x2, Pallas kernels: 12.2 us -> 14.1 us  [the longest x1 7.93 us: denoise_far(): pl.pallas_call(far_kernel, out_shape=(shape, shape), in_specs=[SMEM] + [V...]
  transfers between devices with their start and end apart: 33 -> 33, of which waited for: 12 -> 9; matrix products, arithmetic and copies ran while one was open for 3% -> 3% of each run, Pallas kernels for 9% -> 9%
where the time goes in v1:
time: 171 us
  starting transfers between devices  66.6 us (39%)
  waiting for transfers between devices  52.9 us (31%)
  Pallas kernels  40.3 us (24%)
  local copies, waits for them, and re-layouts  6.32 us (4%)
  other arithmetic  2.51 us (1%)
    ppermute x30, waiting for transfers between devices, send(): lax.ppermute(blocks[k], 'slc', [(i, (i + k) % n) for i in range(n)])  50.2 us
    ppermute x30, starting transfers between devices, send(): lax.ppermute(blocks[k], 'slc', [(i, (i + k) % n) for i in range(n)])  49.1 us
    all_to_all x3, starting transfers between devices, swap(): lax.all_to_all(blocks, 'slc', split_axis=0, concat_axis=0, tiled=True)  17.5 us
    pallas_call x1, Pallas kernels, point_step(): pl.pallas_call(point_kernel, out_shape=[jax.ShapeDtypeStruct((n, *block),...  11.2 us
    pallas_call x2, Pallas kernels, data_step(): pl.pallas_call(kernel, out_shape=jax.ShapeDtypeStruct((n, 2, depth_cols +...  10.8 us
    pallas_call x1, Pallas kernels, denoise_far(): pl.pallas_call(far_kernel, out_shape=(shape, shape), in_specs=[SMEM] + [V...  7.93 us
    pallas_call x1, Pallas kernels, denoise_near(): pl.pallas_call(near_kernel, out_shape=jax.ShapeDtypeStruct((2, spread - 4...  6.19 us
    pallas_call x1, Pallas kernels, maps_step(): pl.pallas_call(maps_kernel, grid=(coils // MAPS_AT_ONCE,), out_shape=[jax...  4.16 us
  transfers between devices with their start and end apart: 33, of which 9 were waited for; matrix products, arithmetic and copies ran while one was open for 3% of the time, Pallas kernels for 9%

profile of v1, /device:TPU:0, one launch (start us, length us, event | category | flops | bytes accessed | tf_op | source)
XLA Modules:
  0.0 170.7 jit_solution(6619147546654534184)
XLA Ops:
  0.6 1.1 convert_bitcast_fusion.1
  1.9 0.7 copy.40.mask_ref
  2.6 11.2 %shard_map.158 = (bf16[16,16,16,128]{3,2,1,0:T(8,128)(2,1)}, bf16[16,16,128]{2,1,0:T(8,128)(2,1)}, bf16[16,16,128]{2,1,0:T(8,128)(2,1)}, bf16[16,16,128]{2,1,0:T...) custom-call(s32[1]{0:T(128)} %bitcast.place_ref.refs_0_, ...), custom_call_target="tpu_custom_call" | custom-call | tf_op jit(solution)/shard_map/pallas_call | solution.py:142
  13.9 7.6 %all-to-all-start = ((bf16[16,16,16,128]{3,2,1,0:T(8,128)(2,1)}), bf16[16,16,16,128]{3,2,1,0:T(8,128)(2,1)S(1)}, u32[]{:S(2)}, u32[]{:S(2)}) async-start(bf16[16,16,16,128]{3,2,1,0:T(8,128)(2,1)} %get-tuple-element.131), calls=%async_computation | async-start | bytes 2097152 | tf_op jit(solution)/shard_map/all_to_all | solution.py:52
  21.4 4.2 %shard_map.159 = (bf16[2,16,2,8,128]{4,3,2,1,0:T(8,128)(2,1)}, bf16[2,16,2,8,128]{4,3,2,1,0:T(8,128)(2,1)}, bf16[2,16,2,8,128]{4,3,2,1,0:T(8,128)(2,1)}, bf16[2,...) custom-call(s32[1]{0:T(128)} %bitcast.place_ref.refs_0_, ...), custom_call_target="tpu_custom_call" | custom-call | tf_op jit(solution)/shard_map/pallas_call | solution.py:84
  25.6 2.9 %collective-permute-start = (bf16[2,16,2,8,128]{4,3,2,1,0:T(8,128)(2,1)}, bf16[2,16,2,8,128]{4,3,2,1,0:T(8,128)(2,1)S(1)}, u32[]{:S(2)}, u32[]{:S(2)}) collective-permute-start(bf16[2,16,2,8,128]{4,3,2,1,0:T(8,128)(2,1)} %get-tuple-element.100), channel_id=1, source_target_pairs={{0,8},{1,9},{2,10},{3,11},{4,12},{5,13},{6,14},{7,15},{8,0},{9,1},... | collective-permute-start | bytes 393224 | tf_op jit(solution)/shard_map/ppermute | solution.py:456
  28.5 1.8 %collective-permute-start.1 = (bf16[2,16,2,8,128]{4,3,2,1,0:T(8,128)(2,1)}, bf16[2,16,2,8,128]{4,3,2,1,0:T(8,128)(2,1)S(1)}, u32[]{:S(2)}, u32[]{:S(2)}) collective-permute-start(bf16[2,16,2,8,128]{4,3,2,1,0:T(8,128)(2,1)} %get-tuple-element.101), channel_id=1, source_target_pairs={{0,7},{1,8},{2,9},{3,10},{4,11},{5,12},{6,13},{7,14},{8,15},{9,0},... | collective-permute-start | bytes 393224 | tf_op jit(solution)/shard_map/ppermute | solution.py:456
  30.3 0.8 collective-permute-start.2
  31.1 2.4 %collective-permute-start.3 = (bf16[2,16,2,8,128]{4,3,2,1,0:T(8,128)(2,1)}, bf16[2,16,2,8,128]{4,3,2,1,0:T(8,128)(2,1)S(1)}, u32[]{:S(2)}, u32[]{:S(2)}) collective-permute-start(bf16[2,16,2,8,128]{4,3,2,1,0:T(8,128)(2,1)} %get-tuple-element.103), channel_id=1, source_target_pairs={{0,6},{1,7},{2,8},{3,9},{4,10},{5,11},{6,12},{7,13},{8,14},{9,15},... | collective-permute-start | bytes 393224 | tf_op jit(solution)/shard_map/ppermute | solution.py:456
  33.5 1.5 collective-permute-start.4
  35.9 29.5 %collective-permute-done.refs_8_.refs_15_ = bf16[2,16,2,8,128]{4,3,2,1,0:T(8,128)(2,1)S(1)} collective-permute-done((bf16[2,16,2,8,128]{4,3,2,1,0:T(8,128)(2,1)}, bf16[2,16,2,8,128]{4,3,2,1,0:T(8,128)(2,1)S(1)}, u32[]{:S(2)}, u32[]{:S(2)}) %collective-permute-start) | collective-permute-done | bytes 131104 | tf_op jit(solution)/shard_map/ppermute | solution.py:456
  65.4 1.7 collective-permute-done.1.refs_7_.refs_14_
  67.0 1.9 %collective-permute-start.6 = (bf16[2,16,2,8,128]{4,3,2,1,0:T(8,128)(2,1)}, bf16[2,16,2,8,128]{4,3,2,1,0:T(8,128)(2,1)S(1)}, u32[]{:S(2)}, u32[]{:S(2)}) collective-permute-start(bf16[2,16,2,8,128]{4,3,2,1,0:T(8,128)(2,1)} %get-tuple-element.106), channel_id=1, source_target_pairs={{0,11},{1,12},{2,13},{3,14},{4,15},{5,0},{6,1},{7,2},{8,3},{9,4},{... | collective-permute-start | bytes 393224 | tf_op jit(solution)/shard_map/ppermute | solution.py:456
  68.9 4.4 %collective-permute-done.3.refs_6_.refs_13_ = bf16[2,16,2,8,128]{4,3,2,1,0:T(8,128)(2,1)S(1)} collective-permute-done((bf16[2,16,2,8,128]{4,3,2,1,0:T(8,128)(2,1)}, bf16[2,16,2,8,128]{4,3,2,1,0:T(8,128)(2,1)S(1)}, u32[]{:S(2)}, u32[]{:S(2)}) %collective-permute-start.3) | collective-permute-done | bytes 131104 | tf_op jit(solution)/shard_map/ppermute | solution.py:456
  73.3 7.1 %collective-permute-start.8 = (bf16[2,16,2,8,128]{4,3,2,1,0:T(8,128)(2,1)}, bf16[2,16,2,8,128]{4,3,2,1,0:T(8,128)(2,1)S(1)}, u32[]{:S(2)}, u32[]{:S(2)}) collective-permute-start(bf16[2,16,2,8,128]{4,3,2,1,0:T(8,128)(2,1)} %get-tuple-element.108), channel_id=1, source_target_pairs={{0,12},{1,13},{2,14},{3,15},{4,0},{5,1},{6,2},{7,3},{8,4},{9,5},{1... | collective-permute-start | bytes 393224 | tf_op jit(solution)/shard_map/ppermute | solution.py:456
  80.4 0.5 collective-permute-start.9
  80.9 3.1 %collective-permute-start.10 = (bf16[2,16,2,8,128]{4,3,2,1,0:T(8,128)(2,1)}, bf16[2,16,2,8,128]{4,3,2,1,0:T(8,128)(2,1)S(1)}, u32[]{:S(2)}, u32[]{:S(2)}) collective-permute-start(bf16[2,16,2,8,128]{4,3,2,1,0:T(8,128)(2,1)} %get-tuple-element.110), channel_id=1, source_target_pairs={{0,13},{1,14},{2,15},{3,0},{4,1},{5,2},{6,3},{7,4},{8,5},{9,6},{10... | collective-permute-start | bytes 393224 | tf_op jit(solution)/shard_map/ppermute | solution.py:456
  84.1 4.7 %collective-permute-start.12 = (bf16[2,16,2,8,128]{4,3,2,1,0:T(8,128)(2,1)}, bf16[2,16,2,8,128]{4,3,2,1,0:T(8,128)(2,1)}, u32[]{:S(2)}, u32[]{:S(2)}) collective-permute-start(bf16[2,16,2,8,128]{4,3,2,1,0:T(8,128)(2,1)} %get-tuple-element.112), channel_id=1, source_target_pairs={{0,14},{1,15},{2,0},{3,1},{4,2},{5,3},{6,4},{7,5},{8,6},{9,7},{10,... | collective-permute-start | bytes 393224 | tf_op jit(solution)/shard_map/ppermute | solution.py:456
  88.8 4.4 %collective-permute-start.14 = (bf16[2,16,2,8,128]{4,3,2,1,0:T(8,128)(2,1)}, bf16[2,16,2,8,128]{4,3,2,1,0:T(8,128)(2,1)}, u32[]{:S(2)}, u32[]{:S(2)}) collective-permute-start(bf16[2,16,2,8,128]{4,3,2,1,0:T(8,128)(2,1)} %get-tuple-element.130), channel_id=1, source_target_pairs={{0,15},{1,0},{2,1},{3,2},{4,3},{5,4},{6,5},{7,6},{8,7},{9,8},{10,9... | collective-permute-start | bytes 393224 | tf_op jit(solution)/shard_map/ppermute | solution.py:456
  93.3 0.6 pad_add_fusion.base_ref
  94.1 0.8 reshape.100.two_ref
  95.3 0.7 fusion.3.one_ref
  96.1 1.2 broadcast_in_dim.5
  97.4 0.8 copy-done.1
  98.3 5.5 %shard_map.160 = bf16[16,2,24,128]{3,2,1,0:T(8,128)(2,1)} custom-call(s32[1]{0:T(128)} %bitcast.place_ref.refs_0_, f32[16,128,128]{2,1,0:T(8,128)} %bitcast.36, bf16[256,256]{1,0:T(8,128)(2,1)} %constant.37.clone.back_src.refs_2_, bf16[256,256]{1,0:T(8,128)(2,1)} %constant.38.clone.fwd.refs_3_, bf16[256,256]{1,0:T(8,128)(2,1)} %constant.39.clone.back.refs_4_, ...), custom_call_target="tpu_custom_call" | custom-call | tf_op jit(solution)/shard_map/pallas_call | solution.py:240
  103.8 4.8 %all-to-all-start.1 = ((bf16[16,2,24,128]{3,2,1,0:T(8,128)(2,1)}), bf16[16,2,24,128]{3,2,1,0:T(8,128)(2,1)S(1)}, u32[]{:S(2)}, u32[]{:S(2)}) async-start(bf16[16,2,24,128]{3,2,1,0:T(8,128)(2,1)} %shard_map.160), calls=%async_computation.1 | async-start | bytes 393216 | tf_op jit(solution)/shard_map/all_to_all | solution.py:52
  109.0 1.6 collective-permute-start.16
  110.7 2.3 %collective-permute-start.17 = (bf16[16,16,128]{2,1,0:T(8,128)(2,1)S(1)}, bf16[16,16,128]{2,1,0:T(8,128)(2,1)S(1)}, u32[]{:S(2)}, u32[]{:S(2)}) collective-permute-start(bf16[16,16,128]{2,1,0:T(8,128)(2,1)S(1)} %copy-done.47), channel_id=1, source_target_pairs={{0,3},{1,4},{2,5},{3,6},{4,7},{5,8},{6,9},{7,10},{8,11},{9,12},{10... | collective-permute-start | bytes 196616 | tf_op jit(solution)/shard_map/ppermute | solution.py:456
  112.9 1.5 collective-permute-start.18
  114.5 3.9 %collective-permute-done.15.refs_24_ = bf16[16,16,128]{2,1,0:T(8,128)(2,1)S(1)} collective-permute-done((bf16[16,16,128]{2,1,0:T(8,128)(2,1)}, bf16[16,16,128]{2,1,0:T(8,128)(2,1)S(1)}, u32[]{:S(2)}, u32[]{:S(2)}) %collective-permute-start.15) | collective-permute-done | bytes 65568 | tf_op jit(solution)/shard_map/ppermute | solution.py:456
  118.4 1.1 collective-permute-done.16.refs_25_
  119.6 0.6 collective-permute-start.21
  120.1 0.6 collective-permute-start.22
  120.8 2.3 %collective-permute-start.23 = (bf16[16,16,128]{2,1,0:T(8,128)(2,1)S(1)}, bf16[16,16,128]{2,1,0:T(8,128)(2,1)S(1)}, u32[]{:S(2)}, u32[]{:S(2)}) collective-permute-start(bf16[16,16,128]{2,1,0:T(8,128)(2,1)S(1)} %copy-done.41), channel_id=1, source_target_pairs={{0,9},{1,10},{2,11},{3,12},{4,13},{5,14},{6,15},{7,0},{8,1},{9,2},... | collective-permute-start | bytes 196616 | tf_op jit(solution)/shard_map/ppermute | solution.py:456
  123.1 7.1 %collective-permute-done.19.refs_28_ = bf16[16,16,128]{2,1,0:T(8,128)(2,1)S(1)} collective-permute-done((bf16[16,16,128]{2,1,0:T(8,128)(2,1)S(1)}, bf16[16,16,128]{2,1,0:T(8,128)(2,1)S(1)}, u32[]{:S(2)}, u32[]{:S(2)}) %collective-permute-start.19) | collective-permute-done | bytes 65568 | tf_op jit(solution)/shard_map/ppermute | solution.py:456
  130.9 2.8 %collective-permute-start.26 = (bf16[16,16,128]{2,1,0:T(8,128)(2,1)S(1)}, bf16[16,16,128]{2,1,0:T(8,128)(2,1)S(1)}, u32[]{:S(2)}, u32[]{:S(2)}) collective-permute-start(bf16[16,16,128]{2,1,0:T(8,128)(2,1)S(1)} %copy-done.38), channel_id=1, source_target_pairs={{0,12},{1,13},{2,14},{3,15},{4,0},{5,1},{6,2},{7,3},{8,4},{9,5},{1... | collective-permute-start | bytes 196616 | tf_op jit(solution)/shard_map/ppermute | solution.py:456
  133.7 1.3 collective-permute-start.27
  135.1 2.7 %collective-permute-start.28 = (bf16[16,16,128]{2,1,0:T(8,128)(2,1)S(1)}, bf16[16,16,128]{2,1,0:T(8,128)(2,1)S(1)}, u32[]{:S(2)}, u32[]{:S(2)}) collective-permute-start(bf16[16,16,128]{2,1,0:T(8,128)(2,1)S(1)} %copy-done.36), channel_id=1, source_target_pairs={{0,14},{1,15},{2,0},{3,1},{4,2},{5,3},{6,4},{7,5},{8,6},{9,7},{10,... | collective-permute-start | bytes 196616 | tf_op jit(solution)/shard_map/ppermute | solution.py:456
  137.8 1.4 collective-permute-start.29
  139.3 2.1 %collective-permute-done.28.refs_37_ = bf16[16,16,128]{2,1,0:T(8,128)(2,1)S(1)} collective-permute-done((bf16[16,16,128]{2,1,0:T(8,128)(2,1)S(1)}, bf16[16,16,128]{2,1,0:T(8,128)(2,1)S(1)}, u32[]{:S(2)}, u32[]{:S(2)}) %collective-permute-start.28) | collective-permute-done | bytes 65568 | tf_op jit(solution)/shard_map/ppermute | solution.py:456
  141.5 0.5 copy-done.30
  142.0 0.6 copy-done.31
  142.6 5.3 %shard_map.161 = bf16[16,2,24,128]{3,2,1,0:T(8,128)(2,1)} custom-call(s32[1]{0:T(128)} %bitcast.place_ref.refs_0_, f32[16,128,128]{2,1,0:T(8,128)} %bitcast.37, bf16[256,256]{1,0:T(8,128)(2,1)} %constant.37.clone.back_src.refs_2_, bf16[256,256]{1,0:T(8,128)(2,1)} %constant.38.clone.fwd.refs_3_, bf16[256,256]{1,0:T(8,128)(2,1)} %constant.39.clone.back.refs_4_, ...), custom_call_target="tpu_custom_call" | custom-call | tf_op jit(solution)/shard_map/pallas_call | solution.py:240
  148.0 5.1 %all-to-all-start.2 = ((bf16[16,2,24,128]{3,2,1,0:T(8,128)(2,1)}), bf16[16,2,24,128]{3,2,1,0:T(8,128)(2,1)S(1)}, u32[]{:S(2)}, u32[]{:S(2)}) async-start(bf16[16,2,24,128]{3,2,1,0:T(8,128)(2,1)} %shard_map.161), calls=%async_computation.2 | async-start | bytes 393216 | tf_op jit(solution)/shard_map/all_to_all | solution.py:52
  153.1 6.2 %shard_map.162.near_ref = f32[2,2,2,7,8,128]{5,4,3,2,1,0:T(8,128)} custom-call(s32[2]{0:T(128)} %pad_add_fusion.base_ref, bf16[16,2,24,128]{3,2,1,0:T(8,128)(2,1)} %copy-done.2, bf16[256,160]{1,0:T(8,128)(2,1)} %fusion.3.one_ref, bf16[48,768]{1,0:T(8,128)(2,1)} %reshape.100.two_ref), custom_call_target="tpu_custom_call" | custom-call | tf_op jit(solution)/shard_map/pallas_call | solution.py:401
  159.3 2.8 %all-to-all-done.2.wb_ref = bf16[16,2,24,128]{3,2,1,0:T(8,128)(2,1)S(1)} async-done(((bf16[16,2,24,128]{3,2,1,0:T(8,128)(2,1)}), bf16[16,2,24,128]{3,2,1,0:T(8,128)(2,1)S(1)}, u32[]{:S(2)}, u32[]{:S(2)}) %all-to-all-start.2) | async-done | bytes 196640 | tf_op jit(solution)/shard_map/all_to_all | solution.py:52
  162.1 0.7 copy-done.4
  162.8 7.9 %shard_map.163 = (f32[2,2,128,128]{3,2,1,0:T(8,128)}, f32[2,2,128,128]{3,2,1,0:T(8,128)}) custom-call(s32[2]{0:T(128)} %pad_add_fusion.base_ref, bf16[16,2,24,128]{3,2,1,0:T(8,128)(2,1)} %copy-done.2, bf16[16,2,24,128]{3,2,1,0:T(8,128)(2,1)} %copy-done.4, f32[2,2,2,7,8,128]{5,4,3,2,1,0:T(8,128)} %shard_map.162.near_ref, bf16[256,160]{1,0:T(8,128)(2,1)} %fusion.3.one_ref, ...), custom_call_target="tpu_custom_call" | custom-call | tf_op jit(solution)/shard_map/pallas_call | solution.py:416
  (148 shorter events, 3.1 us)
Async XLA Ops:
  0.6 34.4 %copy-start = (bf16[27,2,64]{2,1,0:T(2,128)(2,1)S(1)}, bf16[27,2,64]{2,1,0:T(2,128)(2,1)}, u32[]{:S(2)}) copy-start(bf16[27,2,64]{2,1,0:T(2,128)(2,1)} %param.19) | copy-start | bytes 20740
  13.9 83.4 %all-to-all-start = ((bf16[16,16,16,128]{3,2,1,0:T(8,128)(2,1)}), bf16[16,16,16,128]{3,2,1,0:T(8,128)(2,1)S(1)}, u32[]{:S(2)}, u32[]{:S(2)}) async-start(bf16[16,16,16,128]{3,2,1,0:T(8,128)(2,1)} %get-tuple-element.131), calls=%async_computation | async-start | bytes 2097152 | tf_op jit(solution)/shard_map/all_to_all | solution.py:52
  25.6 39.8 %collective-permute-start = (bf16[2,16,2,8,128]{4,3,2,1,0:T(8,128)(2,1)}, bf16[2,16,2,8,128]{4,3,2,1,0:T(8,128)(2,1)S(1)}, u32[]{:S(2)}, u32[]{:S(2)}) collective-permute-start(bf16[2,16,2,8,128]{4,3,2,1,0:T(8,128)(2,1)} %get-tuple-element.100), channel_id=1, source_target_pairs={{0,8},{1,9},{2,10},{3,11},{4,12},{5,13},{6,14},{7,15},{8,0},{9,1},... | collective-permute-start | bytes 393224 | tf_op jit(solution)/shard_map/ppermute | solution.py:456
  28.5 38.6 %collective-permute-start.1 = (bf16[2,16,2,8,128]{4,3,2,1,0:T(8,128)(2,1)}, bf16[2,16,2,8,128]{4,3,2,1,0:T(8,128)(2,1)S(1)}, u32[]{:S(2)}, u32[]{:S(2)}) collective-permute-start(bf16[2,16,2,8,128]{4,3,2,1,0:T(8,128)(2,1)} %get-tuple-element.101), channel_id=1, source_target_pairs={{0,7},{1,8},{2,9},{3,10},{4,11},{5,12},{6,13},{7,14},{8,15},{9,0},... | collective-permute-start | bytes 393224 | tf_op jit(solution)/shard_map/ppermute | solution.py:456
  30.3 38.6 %collective-permute-start.2 = (bf16[2,16,2,8,128]{4,3,2,1,0:T(8,128)(2,1)}, bf16[2,16,2,8,128]{4,3,2,1,0:T(8,128)(2,1)S(1)}, u32[]{:S(2)}, u32[]{:S(2)}) collective-permute-start(bf16[2,16,2,8,128]{4,3,2,1,0:T(8,128)(2,1)} %get-tuple-element.102), channel_id=1, source_target_pairs={{0,9},{1,10},{2,11},{3,12},{4,13},{5,14},{6,15},{7,0},{8,1},{9,2},... | collective-permute-start | bytes 393224 | tf_op jit(solution)/shard_map/ppermute | solution.py:456
  31.1 42.2 %collective-permute-start.3 = (bf16[2,16,2,8,128]{4,3,2,1,0:T(8,128)(2,1)}, bf16[2,16,2,8,128]{4,3,2,1,0:T(8,128)(2,1)S(1)}, u32[]{:S(2)}, u32[]{:S(2)}) collective-permute-start(bf16[2,16,2,8,128]{4,3,2,1,0:T(8,128)(2,1)} %get-tuple-element.103), channel_id=1, source_target_pairs={{0,6},{1,7},{2,8},{3,9},{4,10},{5,11},{6,12},{7,13},{8,14},{9,15},... | collective-permute-start | bytes 393224 | tf_op jit(solution)/shard_map/ppermute | solution.py:456
  33.5 46.9 %collective-permute-start.4 = (bf16[2,16,2,8,128]{4,3,2,1,0:T(8,128)(2,1)}, bf16[2,16,2,8,128]{4,3,2,1,0:T(8,128)(2,1)S(1)}, u32[]{:S(2)}, u32[]{:S(2)}) collective-permute-start(bf16[2,16,2,8,128]{4,3,2,1,0:T(8,128)(2,1)} %get-tuple-element.104), channel_id=1, source_target_pairs={{0,10},{1,11},{2,12},{3,13},{4,14},{5,15},{6,0},{7,1},{8,2},{9,3},... | collective-permute-start | bytes 393224 | tf_op jit(solution)/shard_map/ppermute | solution.py:456
  65.4 31.9 %copy-start.5 = (bf16[2,16,2,8,128]{4,3,2,1,0:T(8,128)(2,1)}, bf16[2,16,2,8,128]{4,3,2,1,0:T(8,128)(2,1)S(1)}, u32[]{:S(2)}) copy-start(bf16[2,16,2,8,128]{4,3,2,1,0:T(8,128)(2,1)S(1)} %collective-permute-done.refs_8_.refs_15_) | copy-start | bytes 393220
  65.4 15.6 %collective-permute-start.5 = (bf16[2,16,2,8,128]{4,3,2,1,0:T(8,128)(2,1)}, bf16[2,16,2,8,128]{4,3,2,1,0:T(8,128)(2,1)S(1)}, u32[]{:S(2)}, u32[]{:S(2)}) collective-permute-start(bf16[2,16,2,8,128]{4,3,2,1,0:T(8,128)(2,1)} %get-tuple-element.105), channel_id=1, source_target_pairs={{0,5},{1,6},{2,7},{3,8},{4,9},{5,10},{6,11},{7,12},{8,13},{9,14},{... | collective-permute-start | bytes 393224 | tf_op jit(solution)/shard_map/ppermute | solution.py:456
  67.0 30.2 %copy-start.6 = (bf16[2,16,2,8,128]{4,3,2,1,0:T(8,128)(2,1)}, bf16[2,16,2,8,128]{4,3,2,1,0:T(8,128)(2,1)S(1)}, u32[]{:S(2)}) copy-start(bf16[2,16,2,8,128]{4,3,2,1,0:T(8,128)(2,1)S(1)} %collective-permute-done.1.refs_7_.refs_14_) | copy-start | bytes 393220
  67.0 17.0 %collective-permute-start.6 = (bf16[2,16,2,8,128]{4,3,2,1,0:T(8,128)(2,1)}, bf16[2,16,2,8,128]{4,3,2,1,0:T(8,128)(2,1)S(1)}, u32[]{:S(2)}, u32[]{:S(2)}) collective-permute-start(bf16[2,16,2,8,128]{4,3,2,1,0:T(8,128)(2,1)} %get-tuple-element.106), channel_id=1, source_target_pairs={{0,11},{1,12},{2,13},{3,14},{4,15},{5,0},{6,1},{7,2},{8,3},{9,4},{... | collective-permute-start | bytes 393224 | tf_op jit(solution)/shard_map/ppermute | solution.py:456
  68.9 28.4 %copy-start.7 = (bf16[2,16,2,8,128]{4,3,2,1,0:T(8,128)(2,1)}, bf16[2,16,2,8,128]{4,3,2,1,0:T(8,128)(2,1)S(1)}, u32[]{:S(2)}) copy-start(bf16[2,16,2,8,128]{4,3,2,1,0:T(8,128)(2,1)S(1)} %collective-permute-done.2.refs_9_.refs_16_) | copy-start | bytes 393220
  68.9 15.1 %collective-permute-start.7 = (bf16[2,16,2,8,128]{4,3,2,1,0:T(8,128)(2,1)}, bf16[2,16,2,8,128]{4,3,2,1,0:T(8,128)(2,1)S(1)}, u32[]{:S(2)}, u32[]{:S(2)}) collective-permute-start(bf16[2,16,2,8,128]{4,3,2,1,0:T(8,128)(2,1)} %get-tuple-element.107), channel_id=1, source_target_pairs={{0,4},{1,5},{2,6},{3,7},{4,8},{5,9},{6,10},{7,11},{8,12},{9,13},{1... | collective-permute-start | bytes 393224 | tf_op jit(solution)/shard_map/ppermute | solution.py:456
  73.3 24.0 %copy-start.8 = (bf16[2,16,2,8,128]{4,3,2,1,0:T(8,128)(2,1)}, bf16[2,16,2,8,128]{4,3,2,1,0:T(8,128)(2,1)S(1)}, u32[]{:S(2)}) copy-start(bf16[2,16,2,8,128]{4,3,2,1,0:T(8,128)(2,1)S(1)} %collective-permute-done.3.refs_6_.refs_13_) | copy-start | bytes 393220
  73.3 15.5 %collective-permute-start.8 = (bf16[2,16,2,8,128]{4,3,2,1,0:T(8,128)(2,1)}, bf16[2,16,2,8,128]{4,3,2,1,0:T(8,128)(2,1)S(1)}, u32[]{:S(2)}, u32[]{:S(2)}) collective-permute-start(bf16[2,16,2,8,128]{4,3,2,1,0:T(8,128)(2,1)} %get-tuple-element.108), channel_id=1, source_target_pairs={{0,12},{1,13},{2,14},{3,15},{4,0},{5,1},{6,2},{7,3},{8,4},{9,5},{1... | collective-permute-start | bytes 393224 | tf_op jit(solution)/shard_map/ppermute | solution.py:456
  80.4 8.4 %collective-permute-start.9 = (bf16[2,16,2,8,128]{4,3,2,1,0:T(8,128)(2,1)}, bf16[2,16,2,8,128]{4,3,2,1,0:T(8,128)(2,1)S(1)}, u32[]{:S(2)}, u32[]{:S(2)}) collective-permute-start(bf16[2,16,2,8,128]{4,3,2,1,0:T(8,128)(2,1)} %get-tuple-element.109), channel_id=1, source_target_pairs={{0,3},{1,4},{2,5},{3,6},{4,7},{5,8},{6,9},{7,10},{8,11},{9,12},{10... | collective-permute-start | bytes 393224 | tf_op jit(solution)/shard_map/ppermute | solution.py:456
  80.9 15.1 %collective-permute-start.10 = (bf16[2,16,2,8,128]{4,3,2,1,0:T(8,128)(2,1)}, bf16[2,16,2,8,128]{4,3,2,1,0:T(8,128)(2,1)S(1)}, u32[]{:S(2)}, u32[]{:S(2)}) collective-permute-start(bf16[2,16,2,8,128]{4,3,2,1,0:T(8,128)(2,1)} %get-tuple-element.110), channel_id=1, source_target_pairs={{0,13},{1,14},{2,15},{3,0},{4,1},{5,2},{6,3},{7,4},{8,5},{9,6},{10... | collective-permute-start | bytes 393224 | tf_op jit(solution)/shard_map/ppermute | solution.py:456
  84.1 12.0 %collective-permute-start.11 = (bf16[2,16,2,8,128]{4,3,2,1,0:T(8,128)(2,1)}, bf16[2,16,2,8,128]{4,3,2,1,0:T(8,128)(2,1)S(1)}, u32[]{:S(2)}, u32[]{:S(2)}) collective-permute-start(bf16[2,16,2,8,128]{4,3,2,1,0:T(8,128)(2,1)} %get-tuple-element.111), channel_id=1, source_target_pairs={{0,2},{1,3},{2,4},{3,5},{4,6},{5,7},{6,8},{7,9},{8,10},{9,11},{10,... | collective-permute-start | bytes 393224 | tf_op jit(solution)/shard_map/ppermute | solution.py:456
  84.1 12.0 %collective-permute-start.12 = (bf16[2,16,2,8,128]{4,3,2,1,0:T(8,128)(2,1)}, bf16[2,16,2,8,128]{4,3,2,1,0:T(8,128)(2,1)}, u32[]{:S(2)}, u32[]{:S(2)}) collective-permute-start(bf16[2,16,2,8,128]{4,3,2,1,0:T(8,128)(2,1)} %get-tuple-element.112), channel_id=1, source_target_pairs={{0,14},{1,15},{2,0},{3,1},{4,2},{5,3},{6,4},{7,5},{8,6},{9,7},{10,... | collective-permute-start | bytes 393224 | tf_op jit(solution)/shard_map/ppermute | solution.py:456
  88.8 8.4 %collective-permute-start.13 = (bf16[2,16,2,8,128]{4,3,2,1,0:T(8,128)(2,1)}, bf16[2,16,2,8,128]{4,3,2,1,0:T(8,128)(2,1)}, u32[]{:S(2)}, u32[]{:S(2)}) collective-permute-start(bf16[2,16,2,8,128]{4,3,2,1,0:T(8,128)(2,1)} %get-tuple-element.116), channel_id=1, source_target_pairs={{0,1},{1,2},{2,3},{3,4},{4,5},{5,6},{6,7},{7,8},{8,9},{9,10},{10,1... | collective-permute-start | bytes 393224 | tf_op jit(solution)/shard_map/ppermute | solution.py:456
  88.8 8.4 %collective-permute-start.14 = (bf16[2,16,2,8,128]{4,3,2,1,0:T(8,128)(2,1)}, bf16[2,16,2,8,128]{4,3,2,1,0:T(8,128)(2,1)}, u32[]{:S(2)}, u32[]{:S(2)}) collective-permute-start(bf16[2,16,2,8,128]{4,3,2,1,0:T(8,128)(2,1)} %get-tuple-element.130), channel_id=1, source_target_pairs={{0,15},{1,0},{2,1},{3,2},{4,3},{5,4},{6,5},{7,6},{8,7},{9,8},{10,9... | collective-permute-start | bytes 393224 | tf_op jit(solution)/shard_map/ppermute | solution.py:456
  98.3 21.9 %copy-start.42 = (bf16[16,16,128]{2,1,0:T(8,128)(2,1)S(1)}, bf16[16,16,128]{2,1,0:T(8,128)(2,1)}, u32[]{:S(2)}) copy-start(bf16[16,16,128]{2,1,0:T(8,128)(2,1)} %get-tuple-element.140) | copy-start | bytes 196612
  98.3 22.5 %copy-start.41 = (bf16[16,16,128]{2,1,0:T(8,128)(2,1)S(1)}, bf16[16,16,128]{2,1,0:T(8,128)(2,1)}, u32[]{:S(2)}) copy-start(bf16[16,16,128]{2,1,0:T(8,128)(2,1)} %get-tuple-element.141) | copy-start | bytes 196612
  98.3 31.9 %copy-start.40 = (bf16[16,16,128]{2,1,0:T(8,128)(2,1)S(1)}, bf16[16,16,128]{2,1,0:T(8,128)(2,1)}, u32[]{:S(2)}) copy-start(bf16[16,16,128]{2,1,0:T(8,128)(2,1)} %get-tuple-element.142) | copy-start | bytes 196612
  98.3 32.2 %copy-start.39 = (bf16[16,16,128]{2,1,0:T(8,128)(2,1)S(1)}, bf16[16,16,128]{2,1,0:T(8,128)(2,1)}, u32[]{:S(2)}) copy-start(bf16[16,16,128]{2,1,0:T(8,128)(2,1)} %get-tuple-element.143) | copy-start | bytes 196612
  98.3 32.6 %copy-start.38 = (bf16[16,16,128]{2,1,0:T(8,128)(2,1)S(1)}, bf16[16,16,128]{2,1,0:T(8,128)(2,1)}, u32[]{:S(2)}) copy-start(bf16[16,16,128]{2,1,0:T(8,128)(2,1)} %get-tuple-element.144) | copy-start | bytes 196612
  98.3 35.4 %copy-start.37 = (bf16[16,16,128]{2,1,0:T(8,128)(2,1)S(1)}, bf16[16,16,128]{2,1,0:T(8,128)(2,1)}, u32[]{:S(2)}) copy-start(bf16[16,16,128]{2,1,0:T(8,128)(2,1)} %get-tuple-element.145) | copy-start | bytes 196612
  98.3 36.8 %copy-start.36 = (bf16[16,16,128]{2,1,0:T(8,128)(2,1)S(1)}, bf16[16,16,128]{2,1,0:T(8,128)(2,1)}, u32[]{:S(2)}) copy-start(bf16[16,16,128]{2,1,0:T(8,128)(2,1)} %get-tuple-element.146) | copy-start | bytes 196612
  98.3 39.5 %copy-start.35 = (bf16[16,16,128]{2,1,0:T(8,128)(2,1)S(1)}, bf16[16,16,128]{2,1,0:T(8,128)(2,1)}, u32[]{:S(2)}) copy-start(bf16[16,16,128]{2,1,0:T(8,128)(2,1)} %get-tuple-element.147) | copy-start | bytes 196612
  103.8 44.1 %all-to-all-start.1 = ((bf16[16,2,24,128]{3,2,1,0:T(8,128)(2,1)}), bf16[16,2,24,128]{3,2,1,0:T(8,128)(2,1)S(1)}, u32[]{:S(2)}, u32[]{:S(2)}) async-start(bf16[16,2,24,128]{3,2,1,0:T(8,128)(2,1)} %shard_map.160), calls=%async_computation.1 | async-start | bytes 393216 | tf_op jit(solution)/shard_map/all_to_all | solution.py:52
  108.6 9.8 %collective-permute-start.15 = (bf16[16,16,128]{2,1,0:T(8,128)(2,1)}, bf16[16,16,128]{2,1,0:T(8,128)(2,1)S(1)}, u32[]{:S(2)}, u32[]{:S(2)}) collective-permute-start(bf16[16,16,128]{2,1,0:T(8,128)(2,1)} %get-tuple-element.133), channel_id=1, source_target_pairs={{0,1},{1,2},{2,3},{3,4},{4,5},{5,6},{6,7},{7,8},{8,9},{9,10},{10,1... | collective-permute-start | bytes 196616 | tf_op jit(solution)/shard_map/ppermute | solution.py:456
  109.0 10.5 %collective-permute-start.16 = (bf16[16,16,128]{2,1,0:T(8,128)(2,1)S(1)}, bf16[16,16,128]{2,1,0:T(8,128)(2,1)S(1)}, u32[]{:S(2)}, u32[]{:S(2)}) collective-permute-start(bf16[16,16,128]{2,1,0:T(8,128)(2,1)S(1)} %copy-done.48), channel_id=1, source_target_pairs={{0,2},{1,3},{2,4},{3,5},{4,6},{5,7},{6,8},{7,9},{8,10},{9,11},{10,... | collective-permute-start | bytes 196616 | tf_op jit(solution)/shard_map/ppermute | solution.py:456
  110.7 9.5 %collective-permute-start.17 = (bf16[16,16,128]{2,1,0:T(8,128)(2,1)S(1)}, bf16[16,16,128]{2,1,0:T(8,128)(2,1)S(1)}, u32[]{:S(2)}, u32[]{:S(2)}) collective-permute-start(bf16[16,16,128]{2,1,0:T(8,128)(2,1)S(1)} %copy-done.47), channel_id=1, source_target_pairs={{0,3},{1,4},{2,5},{3,6},{4,7},{5,8},{6,9},{7,10},{8,11},{9,12},{10... | collective-permute-start | bytes 196616 | tf_op jit(solution)/shard_map/ppermute | solution.py:456
  112.9 7.8 %collective-permute-start.18 = (bf16[16,16,128]{2,1,0:T(8,128)(2,1)S(1)}, bf16[16,16,128]{2,1,0:T(8,128)(2,1)S(1)}, u32[]{:S(2)}, u32[]{:S(2)}) collective-permute-start(bf16[16,16,128]{2,1,0:T(8,128)(2,1)S(1)} %copy-done.46), channel_id=1, source_target_pairs={{0,4},{1,5},{2,6},{3,7},{4,8},{5,9},{6,10},{7,11},{8,12},{9,13},{1... | collective-permute-start | bytes 196616 | tf_op jit(solution)/shard_map/ppermute | solution.py:456
  114.4 15.8 %collective-permute-start.19 = (bf16[16,16,128]{2,1,0:T(8,128)(2,1)S(1)}, bf16[16,16,128]{2,1,0:T(8,128)(2,1)S(1)}, u32[]{:S(2)}, u32[]{:S(2)}) collective-permute-start(bf16[16,16,128]{2,1,0:T(8,128)(2,1)S(1)} %copy-done.45), channel_id=1, source_target_pairs={{0,5},{1,6},{2,7},{3,8},{4,9},{5,10},{6,11},{7,12},{8,13},{9,14},{... | collective-permute-start | bytes 196616 | tf_op jit(solution)/shard_map/ppermute | solution.py:456
  118.4 23.0 %copy-start.17 = (bf16[16,16,128]{2,1,0:T(8,128)(2,1)}, bf16[16,16,128]{2,1,0:T(8,128)(2,1)S(1)}, u32[]{:S(2)}) copy-start(bf16[16,16,128]{2,1,0:T(8,128)(2,1)S(1)} %collective-permute-done.15.refs_24_) | copy-start | bytes 196612
  118.4 12.1 %collective-permute-start.20 = (bf16[16,16,128]{2,1,0:T(8,128)(2,1)S(1)}, bf16[16,16,128]{2,1,0:T(8,128)(2,1)S(1)}, u32[]{:S(2)}, u32[]{:S(2)}) collective-permute-start(bf16[16,16,128]{2,1,0:T(8,128)(2,1)S(1)} %copy-done.44), channel_id=1, source_target_pairs={{0,6},{1,7},{2,8},{3,9},{4,10},{5,11},{6,12},{7,13},{8,14},{9,15},... | collective-permute-start | bytes 196616 | tf_op jit(solution)/shard_map/ppermute | solution.py:456
  119.6 21.9 %copy-start.18 = (bf16[16,16,128]{2,1,0:T(8,128)(2,1)}, bf16[16,16,128]{2,1,0:T(8,128)(2,1)S(1)}, u32[]{:S(2)}) copy-start(bf16[16,16,128]{2,1,0:T(8,128)(2,1)S(1)} %collective-permute-done.16.refs_25_) | copy-start | bytes 196612
  119.6 11.3 %collective-permute-start.21 = (bf16[16,16,128]{2,1,0:T(8,128)(2,1)S(1)}, bf16[16,16,128]{2,1,0:T(8,128)(2,1)S(1)}, u32[]{:S(2)}, u32[]{:S(2)}) collective-permute-start(bf16[16,16,128]{2,1,0:T(8,128)(2,1)S(1)} %copy-done.43), channel_id=1, source_target_pairs={{0,7},{1,8},{2,9},{3,10},{4,11},{5,12},{6,13},{7,14},{8,15},{9,0},... | collective-permute-start | bytes 196616 | tf_op jit(solution)/shard_map/ppermute | solution.py:456
  120.1 13.6 %collective-permute-start.22 = (bf16[16,16,128]{2,1,0:T(8,128)(2,1)S(1)}, bf16[16,16,128]{2,1,0:T(8,128)(2,1)S(1)}, u32[]{:S(2)}, u32[]{:S(2)}) collective-permute-start(bf16[16,16,128]{2,1,0:T(8,128)(2,1)S(1)} %copy-done.42), channel_id=1, source_target_pairs={{0,8},{1,9},{2,10},{3,11},{4,12},{5,13},{6,14},{7,15},{8,0},{9,1},... | collective-permute-start | bytes 196616 | tf_op jit(solution)/shard_map/ppermute | solution.py:456
  120.8 14.3 %collective-permute-start.23 = (bf16[16,16,128]{2,1,0:T(8,128)(2,1)S(1)}, bf16[16,16,128]{2,1,0:T(8,128)(2,1)S(1)}, u32[]{:S(2)}, u32[]{:S(2)}) collective-permute-start(bf16[16,16,128]{2,1,0:T(8,128)(2,1)S(1)} %copy-done.41), channel_id=1, source_target_pairs={{0,9},{1,10},{2,11},{3,12},{4,13},{5,14},{6,15},{7,0},{8,1},{9,2},... | collective-permute-start | bytes 196616 | tf_op jit(solution)/shard_map/ppermute | solution.py:456
  130.2 7.6 %collective-permute-start.24 = (bf16[16,16,128]{2,1,0:T(8,128)(2,1)S(1)}, bf16[16,16,128]{2,1,0:T(8,128)(2,1)S(1)}, u32[]{:S(2)}, u32[]{:S(2)}) collective-permute-start(bf16[16,16,128]{2,1,0:T(8,128)(2,1)S(1)} %copy-done.40), channel_id=1, source_target_pairs={{0,10},{1,11},{2,12},{3,13},{4,14},{5,15},{6,0},{7,1},{8,2},{9,3},... | collective-permute-start | bytes 196616 | tf_op jit(solution)/shard_map/ppermute | solution.py:456
  130.5 8.7 %collective-permute-start.25 = (bf16[16,16,128]{2,1,0:T(8,128)(2,1)S(1)}, bf16[16,16,128]{2,1,0:T(8,128)(2,1)S(1)}, u32[]{:S(2)}, u32[]{:S(2)}) collective-permute-start(bf16[16,16,128]{2,1,0:T(8,128)(2,1)S(1)} %copy-done.39), channel_id=1, source_target_pairs={{0,11},{1,12},{2,13},{3,14},{4,15},{5,0},{6,1},{7,2},{8,3},{9,4},{... | collective-permute-start | bytes 196616 | tf_op jit(solution)/shard_map/ppermute | solution.py:456
  130.9 8.4 %collective-permute-start.26 = (bf16[16,16,128]{2,1,0:T(8,128)(2,1)S(1)}, bf16[16,16,128]{2,1,0:T(8,128)(2,1)S(1)}, u32[]{:S(2)}, u32[]{:S(2)}) collective-permute-start(bf16[16,16,128]{2,1,0:T(8,128)(2,1)S(1)} %copy-done.38), channel_id=1, source_target_pairs={{0,12},{1,13},{2,14},{3,15},{4,0},{5,1},{6,2},{7,3},{8,4},{9,5},{1... | collective-permute-start | bytes 196616 | tf_op jit(solution)/shard_map/ppermute | solution.py:456
  133.7 5.5 %collective-permute-start.27 = (bf16[16,16,128]{2,1,0:T(8,128)(2,1)S(1)}, bf16[16,16,128]{2,1,0:T(8,128)(2,1)S(1)}, u32[]{:S(2)}, u32[]{:S(2)}) collective-permute-start(bf16[16,16,128]{2,1,0:T(8,128)(2,1)S(1)} %copy-done.37), channel_id=1, source_target_pairs={{0,13},{1,14},{2,15},{3,0},{4,1},{5,2},{6,3},{7,4},{8,5},{9,6},{10... | collective-permute-start | bytes 196616 | tf_op jit(solution)/shard_map/ppermute | solution.py:456
  135.1 6.3 %collective-permute-start.28 = (bf16[16,16,128]{2,1,0:T(8,128)(2,1)S(1)}, bf16[16,16,128]{2,1,0:T(8,128)(2,1)S(1)}, u32[]{:S(2)}, u32[]{:S(2)}) collective-permute-start(bf16[16,16,128]{2,1,0:T(8,128)(2,1)S(1)} %copy-done.36), channel_id=1, source_target_pairs={{0,14},{1,15},{2,0},{3,1},{4,2},{5,3},{6,4},{7,5},{8,6},{9,7},{10,... | collective-permute-start | bytes 196616 | tf_op jit(solution)/shard_map/ppermute | solution.py:456
  137.8 3.6 %collective-permute-start.29 = (bf16[16,16,128]{2,1,0:T(8,128)(2,1)S(1)}, bf16[16,16,128]{2,1,0:T(8,128)(2,1)S(1)}, u32[]{:S(2)}, u32[]{:S(2)}) collective-permute-start(bf16[16,16,128]{2,1,0:T(8,128)(2,1)S(1)} %copy-done.35), channel_id=1, source_target_pairs={{0,15},{1,0},{2,1},{3,2},{4,3},{5,4},{6,5},{7,6},{8,7},{9,8},{10,9... | collective-permute-start | bytes 196616 | tf_op jit(solution)/shard_map/ppermute | solution.py:456
  148.0 14.1 %all-to-all-start.2 = ((bf16[16,2,24,128]{3,2,1,0:T(8,128)(2,1)}), bf16[16,2,24,128]{3,2,1,0:T(8,128)(2,1)S(1)}, u32[]{:S(2)}, u32[]{:S(2)}) async-start(bf16[16,2,24,128]{3,2,1,0:T(8,128)(2,1)} %shard_map.161), calls=%async_computation.2 | async-start | bytes 393216 | tf_op jit(solution)/shard_map/all_to_all | solution.py:52
  (34 other events, 367.9 us)
